TPU v7x, 128 devices: a whole 4x4x4 slice. The times are simulated.
128 devices in a mesh: rows: 8 (over y, core), feat: 16 (over z, x).
Axes of the slice: x: 4, y: 4, z: 4, core: 2. Of those that a mesh axis runs over, the one named last changes fastest.
Arguments:
- margins: float32 [24576, 32], P(('rows', 'feat')), may hold values from -30 to 260
- labels: int32 [24576], P(('rows', 'feat')), may hold values from 0 to 31
- row_bins: int32 [1024, 24576], P('feat', 'rows'), may hold values from 0 to 63
- parents: int32 [24576], P('rows'), may hold values from 0 to 7
- split_feature: int32 [8], replicated, may hold values from 0 to 1023
- split_bin: int32 [8], replicated, may hold values from 16 to 47
- leaf_values: float32 [16, 32], replicated, may hold values from -4 to 4
Outputs:
- split_gains: float32 [16, 1024, 64], P('rows', 'feat')
- node_totals: float32 [16, 64], replicated
All inputs are finite; a program needn't handle non-finite values.
Results may differ from a plain program's by a relative error of at most 0.0017.
Values may be sent and summed in bfloat16 or wider, within the bound.
A program may use at most 64 MiB of HBM per device.

v0:
```python
import jax
import jax.numpy as jnp
from jax import lax
from jax.sharding import PartitionSpec as P

BINS = 64


hess_ridge = 1.0


def prefix(value, axis, join, neutral):
    count, mine = (lax.axis_size(axis), lax.axis_index(axis))
    pieces = lax.all_gather(value, axis)
    subtotal = jnp.full_like(value, 0) + jnp.asarray(neutral, value.dtype)

    def turn(position, subtotal):
        longer = join(subtotal, pieces[position])
        return jnp.where(position < mine, longer, subtotal)

    return lax.fori_loop(0, count - 1, turn, subtotal)


def gain_scores(left_sums, totals, classes):
    grad_left = left_sums[..., :classes]
    hess_left = left_sums[..., classes:]
    grad_whole = totals[..., :classes]
    hess_whole = totals[..., classes:]
    grad_right = grad_whole - grad_left
    hess_right = hess_whole - hess_left
    score = (
        grad_left * grad_left / (hess_left + hess_ridge)
        + grad_right * grad_right / (hess_right + hess_ridge)
        - grad_whole * grad_whole / (hess_whole + hess_ridge)
    )
    return jnp.mean(score, axis=-1)


def add_terms(earlier, later):
    return earlier + later


def body(margins, labels, row_bins, parents, split_feature, split_bin, leaf_values):
    feat_dev, group_rows = row_bins.shape
    classes = margins.shape[1]
    node_count = leaf_values.shape[0]
    parent_count = split_feature.shape[0]
    bin_count = BINS
    feat_size = lax.axis_size("feat")
    feat_index = lax.axis_index("feat")
    own_rows = group_rows // feat_size
    parent_hot = parents[:, None] == jnp.arange(parent_count, dtype=jnp.int32)[None, :]
    row_feature = jnp.sum(jnp.where(parent_hot, split_feature[None, :], 0), axis=1)
    row_threshold = jnp.sum(jnp.where(parent_hot, split_bin[None, :], 0), axis=1)
    local_column = row_feature - feat_index * feat_dev
    column_hot = local_column[None, :] == jnp.arange(feat_dev, dtype=jnp.int32)[:, None]
    is_owned = jnp.any(column_hot, axis=0)
    chosen = jnp.sum(jnp.where(column_hot, row_bins, 0), axis=0)
    right_part = jnp.where(is_owned & (chosen > row_threshold), 1.0, 0.0).astype(jnp.float32)
    right_all = lax.psum(right_part.astype(jnp.bfloat16), "feat").astype(jnp.float32)
    node_all = 2 * parents + (right_all > 0.5).astype(jnp.int32)
    node_own = lax.dynamic_slice_in_dim(node_all, feat_index * own_rows, own_rows)
    node_hot_own = (node_own[:, None] == jnp.arange(node_count, dtype=jnp.int32)[None, :]).astype(
        jnp.float32
    )
    logits = margins + jnp.dot(node_hot_own, leaf_values, precision=lax.Precision.HIGHEST)
    probabilities = jax.nn.softmax(logits, axis=1)
    label_hot = (labels[:, None] == jnp.arange(classes, dtype=jnp.int32)[None, :]).astype(
        jnp.float32
    )
    gradient = probabilities - label_hot
    hessian = 2.0 * probabilities * (1.0 - probabilities)
    grad_hess = jnp.concatenate([gradient, hessian], axis=1).astype(jnp.bfloat16)
    partial_totals = lax.dot_general(
        node_hot_own.astype(jnp.bfloat16),
        grad_hess,
        (((0,), (0,)), ((), ())),
        preferred_element_type=jnp.float32,
    )
    node_totals = lax.psum(partial_totals, ("rows", "feat"))
    grad_all = lax.all_gather(grad_hess, "feat", axis=0, tiled=True)
    row_size = lax.axis_size("rows")
    node_hot = node_all[:, None] == jnp.arange(node_count, dtype=jnp.int32)[None, :]
    weighted = jnp.where(node_hot[:, :, None], grad_all[:, None, :], jnp.zeros((), jnp.bfloat16))
    flat_weighted = weighted.reshape(group_rows, node_count * 2 * classes)
    own_bins = bin_count // row_size
    span_rows = own_bins * feat_dev * lax.axis_size("rows")
    bin_span = span_rows // feat_dev
    bin_group = 8

    def one_group(offset):
        values = offset + jnp.arange(bin_group, dtype=jnp.int32)
        one_hot = (row_bins[None, :, :] == values[:, None, None]).astype(jnp.bfloat16)
        one_hot = one_hot.reshape(bin_group * feat_dev, group_rows)
        return jnp.dot(one_hot, flat_weighted, preferred_element_type=jnp.float32)

    blocks = lax.map(one_group, jnp.arange(0, bin_span, bin_group, dtype=jnp.int32))
    own_hist = lax.psum_scatter(
        blocks.reshape(span_rows, node_count * 2 * classes), "rows", scatter_dimension=0, tiled=True
    )
    shaped = own_hist.reshape(own_bins, feat_dev, node_count, 2 * classes)
    running = jnp.cumsum(shaped, axis=0)
    before = prefix(running[-1], "rows", add_terms, jnp.zeros_like(running[-1]))
    left_sums = running + before[None]
    gains_here = gain_scores(left_sums, node_totals[None, None], classes)
    gains_moved = jnp.transpose(gains_here, (2, 1, 0))
    split_gains = lax.all_to_all(gains_moved, "rows", split_axis=0, concat_axis=2, tiled=True)
    return (split_gains, node_totals)


def solution(mesh):
    return jax.shard_map(
        body,
        mesh=mesh,
        in_specs=(
            P(("rows", "feat"), None),
            P(("rows", "feat")),
            P("feat", "rows"),
            P("rows"),
            P(),
            P(),
            P(),
        ),
        out_specs=(P("rows", "feat", None), P()),
        check_vma=False,
    )
```

profile of v0, /device:TPU:1, one launch (start us, length us, event | category | flops | bytes accessed | tf_op | source)
XLA Modules:
  0.0 346.9 jit_solution(17817556389066161247)
XLA Ops:
  8.3 1.2 select_reduce_fusion
  9.5 35.8 %psum.14 = bf16[3072]{0:T(1024)(128)(2,1)S(1)} all-reduce(bf16[3072]{0:T(1024)(128)(2,1)S(1)} %select_convert_fusion), channel_id=1, replica_groups=mesh['rows'=8,'feat'=16] {'feat'}, use_global_device_ids=true, to_apply=%region_4.5 | all-reduce | flops 3072 | bytes 12288 | tf_op jit(solution)/shard_map/psum | solution.py:60
  48.0 15.7 %all-gather = bf16[16,192,64]{1,2,0:T(8,128)(2,1)S(1)} all-gather(bf16[1,192,64]{1,2,0:T(8,128)(2,1)S(1)} %fusion.8), channel_id=1, replica_groups=mesh['rows'=8,'feat'=16] {'feat'}, dimensions={0}, use_global_device_ids=true | all-gather | bytes 417792 | tf_op jit(solution)/shard_map/all_gather | solution.py:81
  64.6 71.0 %while.25 = (s32[]{:T(128)}, f32[8,512,1024]{2,1,0:T(8,128)}, s32[64,3072]{1,0:T(8,128)}, s32[8]{0:T(128)S(1)}, bf16[3072,64]{0,1:T(8,128)(2,1)S(1)}, /*index=5*/pred[3072,16]{0,1:T(8,128)(4,1)S(1)}, s32[]{:T(128)}) while((s32[]{:T(128)}, f32[8,512,1024]{2,1,0:T(8,128)}, s32[64,3072]{1,0:T(8,128)}, s32[8]{0:T(128)S(1)}, ...), condition=%wide.region_8.9_spmd.clone, body=%wide.region_7.8_spmd.clone.sunk | while | flops 3225944064 | bytes 19063452 | solution.py:97
  66.0 2.0 bitcast_compare_fusion.2
  68.6 4.9 %bitcast_dynamic-update-slice_fusion.2 = f32[8,512,1024]{2,1,0:T(8,128)} fusion(f32[8,512,1024]{2,1,0:T(8,128)} %get-tuple-element.248, s32[]{:T(128)} %get-tuple-element.247, pred[512,3072]{1,0:T(32,128)(4,1)S(1)} %bitcast_compare_fusion.2, bf16[3072,1024]{0,1:T(8,128)(2,1)S(1)} %bitcast.48), kind=kOutput, calls=%fused_computation.3.clone.1 | convolution fusion | flops 3221225472 | bytes 9961984 | tf_op jit(solution)/shard_map/while/body/eval_jaxpr/dot_general | solution.py:95
  74.9 2.0 bitcast_compare_fusion.2
  77.5 4.8 %bitcast_dynamic-update-slice_fusion.2 = f32[8,512,1024]{2,1,0:T(8,128)} fusion(f32[8,512,1024]{2,1,0:T(8,128)} %get-tuple-element.248, s32[]{:T(128)} %get-tuple-element.247, pred[512,3072]{1,0:T(32,128)(4,1)S(1)} %bitcast_compare_fusion.2, bf16[3072,1024]{0,1:T(8,128)(2,1)S(1)} %bitcast.48), kind=kOutput, calls=%fused_computation.3.clone.1 | convolution fusion | flops 3221225472 | bytes 9961984 | tf_op jit(solution)/shard_map/while/body/eval_jaxpr/dot_general | solution.py:95
  83.7 2.0 bitcast_compare_fusion.2
  86.3 4.8 %bitcast_dynamic-update-slice_fusion.2 = f32[8,512,1024]{2,1,0:T(8,128)} fusion(f32[8,512,1024]{2,1,0:T(8,128)} %get-tuple-element.248, s32[]{:T(128)} %get-tuple-element.247, pred[512,3072]{1,0:T(32,128)(4,1)S(1)} %bitcast_compare_fusion.2, bf16[3072,1024]{0,1:T(8,128)(2,1)S(1)} %bitcast.48), kind=kOutput, calls=%fused_computation.3.clone.1 | convolution fusion | flops 3221225472 | bytes 9961984 | tf_op jit(solution)/shard_map/while/body/eval_jaxpr/dot_general | solution.py:95
  92.5 2.0 bitcast_compare_fusion.2
  95.2 4.9 %bitcast_dynamic-update-slice_fusion.2 = f32[8,512,1024]{2,1,0:T(8,128)} fusion(f32[8,512,1024]{2,1,0:T(8,128)} %get-tuple-element.248, s32[]{:T(128)} %get-tuple-element.247, pred[512,3072]{1,0:T(32,128)(4,1)S(1)} %bitcast_compare_fusion.2, bf16[3072,1024]{0,1:T(8,128)(2,1)S(1)} %bitcast.48), kind=kOutput, calls=%fused_computation.3.clone.1 | convolution fusion | flops 3221225472 | bytes 9961984 | tf_op jit(solution)/shard_map/while/body/eval_jaxpr/dot_general | solution.py:95
  101.4 2.0 bitcast_compare_fusion.2
  104.1 4.9 %bitcast_dynamic-update-slice_fusion.2 = f32[8,512,1024]{2,1,0:T(8,128)} fusion(f32[8,512,1024]{2,1,0:T(8,128)} %get-tuple-element.248, s32[]{:T(128)} %get-tuple-element.247, pred[512,3072]{1,0:T(32,128)(4,1)S(1)} %bitcast_compare_fusion.2, bf16[3072,1024]{0,1:T(8,128)(2,1)S(1)} %bitcast.48), kind=kOutput, calls=%fused_computation.3.clone.1 | convolution fusion | flops 3221225472 | bytes 9961984 | tf_op jit(solution)/shard_map/while/body/eval_jaxpr/dot_general | solution.py:95
  110.3 2.0 bitcast_compare_fusion.2
  113.0 4.8 %bitcast_dynamic-update-slice_fusion.2 = f32[8,512,1024]{2,1,0:T(8,128)} fusion(f32[8,512,1024]{2,1,0:T(8,128)} %get-tuple-element.248, s32[]{:T(128)} %get-tuple-element.247, pred[512,3072]{1,0:T(32,128)(4,1)S(1)} %bitcast_compare_fusion.2, bf16[3072,1024]{0,1:T(8,128)(2,1)S(1)} %bitcast.48), kind=kOutput, calls=%fused_computation.3.clone.1 | convolution fusion | flops 3221225472 | bytes 9961984 | tf_op jit(solution)/shard_map/while/body/eval_jaxpr/dot_general | solution.py:95
  119.2 2.0 bitcast_compare_fusion.2
  121.8 4.9 %bitcast_dynamic-update-slice_fusion.2 = f32[8,512,1024]{2,1,0:T(8,128)} fusion(f32[8,512,1024]{2,1,0:T(8,128)} %get-tuple-element.248, s32[]{:T(128)} %get-tuple-element.247, pred[512,3072]{1,0:T(32,128)(4,1)S(1)} %bitcast_compare_fusion.2, bf16[3072,1024]{0,1:T(8,128)(2,1)S(1)} %bitcast.48), kind=kOutput, calls=%fused_computation.3.clone.1 | convolution fusion | flops 3221225472 | bytes 9961984 | tf_op jit(solution)/shard_map/while/body/eval_jaxpr/dot_general | solution.py:95
  128.1 2.0 bitcast_compare_fusion.2
  130.7 4.8 %bitcast_dynamic-update-slice_fusion.2 = f32[8,512,1024]{2,1,0:T(8,128)} fusion(f32[8,512,1024]{2,1,0:T(8,128)} %get-tuple-element.248, s32[]{:T(128)} %get-tuple-element.247, pred[512,3072]{1,0:T(32,128)(4,1)S(1)} %bitcast_compare_fusion.2, bf16[3072,1024]{0,1:T(8,128)(2,1)S(1)} %bitcast.48), kind=kOutput, calls=%fused_computation.3.clone.1 | convolution fusion | flops 3221225472 | bytes 9961984 | tf_op jit(solution)/shard_map/while/body/eval_jaxpr/dot_general | solution.py:95
  135.6 103.8 %reduce-scatter.2.cloned.1.call-done = f32[512,1024]{1,0:T(8,128)} async-done(((f32[4096,1024]{1,0:T(8,128)}), f32[512,1024]{1,0:T(8,128)}) %reduce-scatter.2.cloned.1.call-update) | async-done | bytes 2097168 | tf_op jit(solution)/shard_map/reduce_scatter | solution.py:98
  239.4 4.5 %reshape.57 = f32[8,64,16,64]{3,2,1,0:T(8,128)} reshape(f32[512,1024]{1,0:T(8,128)} %reduce-scatter.2.cloned.1.call-done) | data formatting | bytes 4194304 | tf_op jit(solution)/shard_map/reshape | solution.py:101
  243.9 2.5 fusion.11
  246.4 1.9 copy-done.1
  249.5 66.0 %psum.15 = f32[16,64]{1,0:T(8,128)S(1)} all-reduce(f32[16,64]{1,0:T(8,128)S(1)} %fusion.3), channel_id=1, replica_groups=mesh['rows'=8,'feat'=16] {'rows','feat'}, use_global_device_ids=true, to_apply=%region_13.14 | all-reduce | flops 1024 | bytes 8192 | tf_op jit(solution)/shard_map/psum | solution.py:80
  315.5 8.6 %while.26 = (s32[]{:T(128)}, f32[64,16,64]{2,1,0:T(8,128)S(1)}, s32[]{:T(128)}, f32[8,64,16,64]{3,2,1,0:T(8,128)}, s32[]{:T(128)}, /*index=5*/s32[]{:T(128)}) while((s32[]{:T(128)}, f32[64,16,64]{2,1,0:T(8,128)S(1)}, s32[]{:T(128)}, f32[8,64,16,64]{3,2,1,0:T(8,128)}, s32[]{:T(128)}, /*index=5*/s32[]{:T(128)}) %tuple.64), condition=%wide.region_12.13_spmd.clone, body=%wide.region_11.12_spmd.clone.sunk | while | flops 196612 | bytes 786525 | solution.py:21
  315.6 1.2 add_select_fusion.2
  316.8 1.2 add_select_fusion.2
  319.3 1.2 add_select_fusion.2
  324.2 2.7 broadcast_add_fusion
  326.9 2.8 subtract_reduce_fusion
  329.9 8.1 %all_to_all.18 = f32[8,1,1024]{2,1,0:T(1,128)S(1)} all-to-all(f32[8,1,1024]{2,1,0:T(1,128)S(1)} %reshape.60), channel_id=1, replica_groups=mesh['rows'=8,'feat'=16] {'rows'}, dimensions={0} | all-to-all | bytes 65536 | tf_op jit(solution)/shard_map/all_to_all | solution.py:107
  (81 shorter events, 28.6 us)
Async XLA Ops:
  7.2 39.0 %copy-start = (f32[16,32]{1,0:T(8,128)S(1)}, f32[16,32]{1,0:T(8,128)}, u32[]{:S(2)}) copy-start(f32[16,32]{1,0:T(8,128)} %param.17) | copy-start | bytes 6148
  7.2 232.2 %reduce-scatter.2.cloned.1.call-start = ((), (), s32[]{:S(2)}) async-start(), calls=%async_computation.2 | async-start | bytes 18874368 | tf_op jit(solution)/shard_map/reduce_scatter | solution.py:98
  135.6 180.0 %all-gather.3.cloned.1.call-start = ((), (), s32[]{:S(2)}) async-start(), calls=%async_computation.3 | async-start | bytes 4718592 | tf_op jit(solution)/shard_map/all_gather | solution.py:14
  246.4 1.9 copy-start.1
  315.5 11.4 %copy-start.2 = (f32[16,64]{1,0:T(8,128)}, f32[16,64]{1,0:T(8,128)S(1)}, u32[]{:S(2)}) copy-start(f32[16,64]{1,0:T(8,128)S(1)} %psum.15) | copy-start | bytes 12292
Sparse Core Ops, SparseCore 0:
  135.7 103.6 reduce-scatter.1
  249.3 33.3 all-gather.2
where the time goes:
time: 348 us; the launch traced here: 347 us
  blocking collectives  126 us (36%)
  waiting for transfers between devices  104 us (30%)
  other arithmetic  47.1 us (14%)
  matrix products  40.1 us (12%)
  local copies, waits for them, and re-layouts  15.6 us (4%)
  between operations  14.2 us (4%)
    reduce_scatter x1, waiting for transfers between devices, body(): lax.psum_scatter(blocks.reshape(span_rows, node_count * 2 * classes), 'ro...  104 us
    psum x1, blocking collectives, body(): node_totals = lax.psum(partial_totals, ('rows', 'feat'))  66 us
    dot_general x8, matrix products, one_group(): return jnp.dot(one_hot, flat_weighted, preferred_element_type=jnp.float32)  38.8 us
    psum x1, blocking collectives, body(): lax.psum(right_part.astype(jnp.bfloat16), 'feat').astype(jnp.float32)  35.8 us
    eq x8, other arithmetic, one_group(): row_bins[None, :, :] == values[:, None, None]  16.3 us
    all_gather x1, blocking collectives, body(): grad_all = lax.all_gather(grad_hess, 'feat', axis=0, tiled=True)  15.7 us
    select_n x7, other arithmetic, turn(): return jnp.where(position < mine, longer, subtotal)  8.49 us
    all_to_all x1, blocking collectives, body(): lax.all_to_all(gains_moved, 'rows', split_axis=0, concat_axis=2, tiled=True)  8.11 us
  transfers between devices with their start and end apart: 2, of which 1 were waited for; matrix products, arithmetic and copies ran while one was open for 0% of the time, Pallas kernels for 0%

commit v1 on v0

v1 whole, which is shorter than its diff:
```python
import functools

import jax
import jax.numpy as jnp
from jax import lax
from jax.experimental import pallas as pl
from jax.experimental.pallas import tpu as pltpu
from jax.sharding import PartitionSpec as P

MESH = pl.DeviceIdType.MESH
BINS = 64
NODES = 16
CLASSES = 32
COLS = 2 * CLASSES
PARENTS = 8
RIDGE = 1.0
LANES = 128
NR = 8
NF = 16
OWN = 192
GROUP = 3072
KB = GROUP // LANES
FD = 64
FL = FD // NR
UNIT = 12 * LANES
BF = jnp.bfloat16
F32 = jnp.float32


def own_gradients(margins, labels, parents, leaf_t, side):
    leaf = jnp.zeros(margins.shape, F32)
    for p in range(PARENTS):
        column = leaf_t[:, 2 * p + side : 2 * p + side + 1]
        leaf = jnp.where(parents == p, column, leaf)
    logits = margins + leaf
    top = jnp.max(logits, axis=0, keepdims=True)
    grown = jnp.exp(logits - top)
    prob = grown / jnp.sum(grown, axis=0, keepdims=True)
    classes = lax.broadcasted_iota(jnp.int32, margins.shape, 0)
    hot = jnp.where(classes == labels, 1.0, 0.0)
    return prob - hot, 2.0 * prob * (1.0 - prob)


def kernel(
    sf_ref, sb_ref, margin_ref, label_ref, bins_ref, par_ref, parrow_ref, leaf_ref,
    gain_ref, total_ref,
    bit_f32, bit_send, bit_recv, bin_send, bin_recv, bin_all, node_all,
    grads, weighted, mask, acc, unit_tot, gain_send, gain_recv,
    bit_ss, bit_rs, bin_ss, bin_rs, node_ss, node_rs, y_ss, y_rs, x_ss, x_rs,
    z_ss, z_rs, sib_ss, sib_rs, out_ss, out_rs,
):
    row = lax.axis_index("rows")
    feat = lax.axis_index("feat")
    y, core = row // 2, row % 2
    z, x = feat // 4, feat % 4
    odd = feat % 2
    xo = x // 2

    def send(src, dst, ss, rs, r, f):
        return pltpu.make_async_remote_copy(
            src_ref=src, dst_ref=dst, send_sem=ss, recv_sem=rs,
            device_id=(r, f), device_id_type=MESH,
        )

    barrier = pltpu.get_barrier_semaphore()
    for d in range(1, NF):
        pl.semaphore_signal(barrier, inc=1, device_id=(row, (feat + d) % NF), device_id_type=MESH)
    for d in range(1, NR):
        pl.semaphore_signal(barrier, inc=1, device_id=((row + d) % NR, feat), device_id_type=MESH)

    right = jnp.zeros((1, GROUP), F32)
    for p in range(PARENTS):
        local = sf_ref[p] - feat * FD
        owned = jnp.logical_and(local >= 0, local < FD).astype(jnp.int32)
        at = jnp.minimum(jnp.maximum(local, 0), FD - 1)
        limit = sb_ref[p] * owned + BINS * (1 - owned)
        hit = jnp.logical_and(bins_ref[pl.ds(at, 1), :] > limit, parrow_ref[...] == p)
        right = jnp.where(hit, 1.0, right)
    bit_f32[...] = jnp.zeros_like(bit_f32)
    for k in range(KB):
        bit_f32[k : k + 1, :] = right[:, k * LANES : (k + 1) * LANES]
    bit_send[...] = bit_f32[...].astype(BF)

    pl.semaphore_wait(barrier, NF - 1 + NR - 1)

    def bit_copy(d):
        return send(
            bit_send, bit_recv.at[d], bit_ss.at[d], bit_rs.at[d], row, (feat + d) % NF
        )

    for d in range(1, NF):
        bit_copy(d).start()

    def bin_copy(d):
        to = (row + d) % NR
        return send(bin_send.at[d], bin_recv.at[d], bin_ss.at[d], bin_rs.at[d], to, feat)

    def load_bins(to):
        first = pl.multiple_of(to * FL, FL)
        parts = [
            bins_ref[pl.ds(first, FL), k * LANES : (k + 1) * LANES].astype(F32)
            for k in range(KB)
        ]
        return parts

    for d in range(1, NR):
        parts = load_bins((row + d) % NR)
        bin_send[d] = jnp.concatenate(parts, axis=0).astype(BF)
        bin_copy(d).start()
    for k, part in enumerate(load_bins(row)):
        bin_all[row, k] = part

    pair = feat // 2

    def arrange(value):
        padded = jnp.concatenate(
            [value, jnp.zeros((value.shape[0], 2 * LANES - OWN), value.dtype)], axis=1
        )
        turned = jnp.concatenate(
            [padded[:, 64:], padded[:, :64]], axis=1
        )
        return jnp.where(odd == 1, turned, padded)

    def own_rows(ref):
        main = ref[pl.ds(3 * pair + 2 * odd, 1), :]
        rest = ref[pl.ds(3 * pair + 1, 1), :]
        return jnp.concatenate([main, rest], axis=1)

    margins = arrange(margin_ref[...])
    labels = arrange(label_ref[...])
    own_parents = own_rows(par_ref)
    leaf_t = leaf_ref[...].T
    left_g, left_h = own_gradients(margins, labels, own_parents, leaf_t, 0)
    right_g, right_h = own_gradients(margins, labels, own_parents, leaf_t, 1)

    bits = bit_send[...].astype(F32)
    for d in range(1, NF):
        bit_copy(d).wait_recv()
        bits = bits + bit_recv[d].astype(F32)
    node_all[row] = (2 * par_ref[...]).astype(F32) + bits[:KB]
    bit_f32[...] = bits

    def node_copy(d):
        to = (row + d) % NR
        return send(node_all.at[row], node_all.at[row], node_ss.at[d], node_rs.at[d], to, feat)

    goes_right = own_rows(bit_f32) > 0.5
    g = jnp.where(goes_right, right_g, left_g)
    h = jnp.where(goes_right, right_h, left_h)
    lane = lax.broadcasted_iota(jnp.int32, (CLASSES, LANES), 1)
    first_half = lane < 64
    keep = first_half == (odd == 0)
    rest = jnp.where(keep, g[:, LANES:], pltpu.roll(h[:, LANES:], 64, 1))
    grads[core, z, x, y] = jnp.concatenate(
        [g[:, :LANES], h[:, :LANES], rest], axis=0
    ).astype(BF)

    def y_copy(d):
        to = ((y + d) % 4) * 2 + core
        at = grads.at[core, z, x, y]
        return send(at, at, y_ss.at[d], y_rs.at[d], to, feat)

    for d in range(1, 4):
        y_copy(d).start()
    for d in range(1, NR):
        node_copy(d).start()

    def x_copy(d):
        at = grads.at[core, z, x]
        return send(at, at, x_ss.at[d], x_rs.at[d], row, 4 * z + (x + d) % 4)

    def x_wait(d):
        at = grads.at[core, z, (x + 4 - d) % 4]
        send(at, at, x_ss.at[d], x_rs.at[d], row, feat).wait_recv()

    def unit_at(half, dz, q):
        return grads.at[half, (z + dz) % 4, pl.ds(2 * ((xo + q) % 2), 2)]

    def z_copy(way, q):
        at = unit_at(core, 0, q)
        to = 4 * ((z + 1 + 2 * way) % 4) + x
        return send(at, at, z_ss.at[way, q], z_rs.at[way, q], row, to)

    def z_wait(way, q):
        at = unit_at(core, 3 - 2 * way, q)
        send(at, at, z_ss.at[way, q], z_rs.at[way, q], row, feat).wait_recv()

    def far_copy(q):
        at = unit_at(core, 3 - 2 * q, q)
        to = 4 * ((z + 1 + 2 * q) % 4) + x
        return send(at, at, z_ss.at[2, q], z_rs.at[2, q], row, to)

    def far_wait(q):
        at = unit_at(core, 2, q)
        send(at, at, z_ss.at[2, q], z_rs.at[2, q], row, feat).wait_recv()

    def sib_copy(dz, q):
        at = unit_at(core, dz, q)
        return send(at, at, sib_ss.at[dz, q], sib_rs.at[dz, q], row + 1 - 2 * core, feat)

    def sib_wait(dz, q):
        at = unit_at(1 - core, dz, q)
        send(at, at, sib_ss.at[dz, q], sib_rs.at[dz, q], row, feat).wait_recv()

    for d in range(1, 4):
        at = grads.at[core, z, x, (y + 4 - d) % 4]
        send(at, at, y_ss.at[d], y_rs.at[d], row, feat).wait_recv()
    for d in (1, 3, 2):
        x_copy(d).start()

    acc[...] = jnp.zeros_like(acc)

    for d in range(1, NR):
        bin_copy(d).wait_recv()
        came = (row + NR - d) % NR
        block = bin_recv[d].astype(F32)
        for k in range(KB):
            bin_all[came, k] = block[k * FL : (k + 1) * FL]
    for d in range(1, NR):
        at = node_all.at[(row + NR - d) % NR]
        send(at, at, node_ss.at[d], node_rs.at[d], row, feat).wait_recv()

    @pl.when(odd == 1)
    def _():
        x_wait(1)

    @pl.when(odd == 0)
    def _():
        x_wait(3)

    z_copy(0, 0).start()
    z_copy(1, 0).start()
    sib_copy(0, 0).start()

    lane_low = lax.broadcasted_iota(jnp.int32, (32, LANES), 1) < 64
    bin_ids = lax.broadcasted_iota(jnp.int32, (BINS, LANES), 0).astype(F32).astype(BF)
    node_ids = lax.broadcasted_iota(jnp.int32, (NODES, LANES), 0).astype(F32).astype(BF)

    def unit(u, carry):
        t, rel = u // 2, u % 2
        group, r = t // 2, t % 2
        mid = ((group + 1) // 2) % 2
        q = (1 - mid) * r + mid * (group - 1)
        dz = mid * (3 - 2 * r) + (1 - mid) * 2 * (group // 3)
        half = (core + rel) % 2

        @pl.when(u == 1)
        def _():
            @pl.when(odd == 1)
            def _():
                x_wait(3)

            @pl.when(odd == 0)
            def _():
                x_wait(1)

            x_wait(2)
            z_copy(0, 1).start()
            z_copy(1, 1).start()
            sib_copy(0, 1).start()
            sib_wait(0, 0)

        @pl.when(u == 3)
        def _():
            sib_wait(0, 1)

        @pl.when(u == 4)
        def _():
            z_wait(0, 0)
            far_copy(0).start()
            sib_copy(3, 0).start()
            z_wait(1, 0)
            sib_copy(1, 0).start()

        @pl.when(u == 5)
        def _():
            sib_wait(3, 0)

        @pl.when(u == 6)
        def _():
            z_wait(1, 1)
            far_copy(1).start()
            sib_copy(1, 1).start()
            z_wait(0, 1)
            sib_copy(3, 1).start()

        @pl.when(u == 7)
        def _():
            sib_wait(1, 0)

        @pl.when(u == 9)
        def _():
            sib_wait(3, 1)

        @pl.when(u == 10)
        def _():
            far_wait(0)
            sib_copy(2, 0).start()
            far_wait(1)
            sib_copy(2, 1).start()

        @pl.when(u == 11)
        def _():
            sib_wait(1, 1)

        @pl.when(u == 13)
        def _():
            sib_wait(2, 0)

        @pl.when(u == 15)
        def _():
            sib_wait(2, 1)

        zz = (z + dz) % 4
        xp = (xo + q) % 2
        first = 3 * (2 * zz + xp)
        hots = []
        pieces = []
        for yy in range(4):
            group_row = 2 * yy + half
            even = grads[half, zz, 2 * xp, yy]
            last = grads[half, zz, 2 * xp + 1, yy]
            rest_e, rest_o = even[64:], last[64:]
            low = jnp.where(lane_low, rest_e, rest_o)
            high = jnp.where(lane_low, rest_o, rest_e).astype(F32)
            high = pltpu.roll(high, 64, 1).astype(BF)
            middle = jnp.concatenate([low, high], axis=0)
            for i, piece in enumerate((even[:64], middle, last[:64])):
                at = (yy * 3 + i) * LANES
                nodes = node_all[group_row, pl.ds(first + i, 1), :].astype(BF)
                nodes_g = jnp.broadcast_to(nodes, (COLS, LANES))
                for n in range(NODES):
                    weighted[n * COLS : (n + 1) * COLS, at : at + LANES] = jnp.where(
                        nodes_g == BF(n), piece, jnp.zeros_like(piece)
                    )
                hots.append(
                    jnp.where(
                        jnp.broadcast_to(nodes, (NODES, LANES)) == node_ids, BF(1), BF(0)
                    )
                )
                pieces.append(piece)
                for f in range(FL):
                    here = bin_all[group_row, first + i, f : f + 1, :].astype(BF)
                    mask[f * BINS : (f + 1) * BINS, at : at + LANES] = jnp.where(
                        jnp.broadcast_to(here, (BINS, LANES)) <= bin_ids, BF(1), BF(0)
                    )
        contract = (((1,), (1,)), ((), ()))
        acc[...] += lax.dot_general(
            weighted[...], mask[...], contract, preferred_element_type=F32
        )
        unit_tot[half * 8 + 2 * zz + xp] = lax.dot_general(
            jnp.concatenate(hots, axis=1),
            jnp.concatenate(pieces, axis=1),
            contract,
            preferred_element_type=F32,
        )
        return carry

    lax.fori_loop(0, 16, unit, 0)

    totals = unit_tot[0]
    for u in range(1, 16):
        totals = totals + unit_tot[u]
    total_ref[...] = totals

    for n in range(NODES):
        base = n * COLS
        gl = acc[base : base + CLASSES, :]
        hl = acc[base + CLASSES : base + COLS, :]
        whole_g = acc[base : base + CLASSES, BINS - 1 : BINS]
        whole_h = acc[base + CLASSES : base + COLS, BINS - 1 : BINS]
        gr = whole_g - gl
        hr = whole_h - hl
        score = (
            gl * gl / (hl + RIDGE)
            + gr * gr / (hr + RIDGE)
            - whole_g * whole_g / (whole_h + RIDGE)
        )
        gain = jnp.sum(score, axis=0, keepdims=True) * (1.0 / CLASSES)
        for k in range(4):
            gain_send[n // 2, (n % 2) * 4 + k : (n % 2) * 4 + k + 1, :] = gain[
                :, k * LANES : (k + 1) * LANES
            ]

    def out_copy(d):
        to = (row + d) % NR
        return send(
            gain_send.at[to], gain_recv.at[row], out_ss.at[d], out_rs.at[d], to, feat
        )

    for d in range(1, NR):
        out_copy(d).start()
    gain_ref[row] = gain_send[row]
    for d in range(1, NR):
        came = (row + NR - d) % NR
        at = gain_recv.at[came]
        send(at, at, out_ss.at[d], out_rs.at[d], row, feat).wait_recv()
        gain_ref[came] = gain_recv[came]

    for d in range(1, NF):
        bit_copy(d).wait_send()
    for d in range(1, NR):
        bin_copy(d).wait_send()
        node_copy(d).wait_send()
        out_copy(d).wait_send()
    for d in range(1, 4):
        y_copy(d).wait_send()
        x_copy(d).wait_send()
    for q in range(2):
        for way in range(2):
            z_copy(way, q).wait_send()
        far_copy(q).wait_send()
        for dz in range(4):
            sib_copy(dz, q).wait_send()


def body(margins, labels, row_bins, parents, split_feature, split_bin, leaf_values):
    vmem = pl.BlockSpec(memory_space=pltpu.VMEM)
    smem = pl.BlockSpec(memory_space=pltpu.SMEM)
    dma = pltpu.SemaphoreType.DMA
    gains, totals = pl.pallas_call(
        kernel,
        out_shape=(
            jax.ShapeDtypeStruct((NR, 8, LANES), F32),
            jax.ShapeDtypeStruct((NODES, COLS), F32),
        ),
        in_specs=[smem, smem] + [vmem] * 6,
        out_specs=(vmem, vmem),
        scratch_shapes=[
            pltpu.VMEM((32, LANES), F32),
            pltpu.VMEM((32, LANES), BF),
            pltpu.VMEM((NF, 32, LANES), BF),
            pltpu.VMEM((NR, KB * FL, LANES), BF),
            pltpu.VMEM((NR, KB * FL, LANES), BF),
            pltpu.VMEM((NR, KB, FL, LANES), F32),
            pltpu.VMEM((NR, KB, LANES), F32),
            pltpu.VMEM((2, 4, 4, 4, 96, LANES), BF),
            pltpu.VMEM((NODES * COLS, UNIT), BF),
            pltpu.VMEM((FL * BINS, UNIT), BF),
            pltpu.VMEM((NODES * COLS, FL * BINS), F32),
            pltpu.VMEM((16, NODES, COLS), F32),
            pltpu.VMEM((NR, 8, LANES), F32),
            pltpu.VMEM((NR, 8, LANES), F32),
            dma((NF,)), dma((NF,)), dma((NR,)), dma((NR,)), dma((NR,)), dma((NR,)),
            dma((4,)), dma((4,)), dma((4,)), dma((4,)),
            dma((3, 2)), dma((3, 2)), dma((4, 2)), dma((4, 2)),
            dma((NR,)), dma((NR,)),
        ],
        compiler_params=pltpu.CompilerParams(
            collective_id=0, has_side_effects=True, vmem_limit_bytes=48 << 20
        ),
    )(
        split_feature,
        split_bin,
        margins.T,
        labels.reshape(1, OWN),
        row_bins,
        parents.reshape(KB, LANES),
        parents.reshape(1, GROUP),
        leaf_values,
    )
    shaped = gains.reshape(NR, 2, 4, 2, BINS).transpose(1, 0, 2, 3, 4)
    return shaped.reshape(2, FD, BINS), totals


def solution(mesh):
    return jax.shard_map(
        body,
        mesh=mesh,
        in_specs=(
            P(("rows", "feat"), None),
            P(("rows", "feat")),
            P("feat", "rows"),
            P("rows"),
            P(),
            P(),
            P(),
        ),
        out_specs=(P("rows", "feat", None), P()),
        check_vma=False,
    )
```

time: 348 us -> 67.4 us (0.19)
  blocking collectives: 126 us -> 0 us
  waiting for transfers between devices: 104 us -> 0 us
  Pallas kernels: 0 us -> 61.1 us
  other arithmetic: 47.1 us -> 0 us
  matrix products: 40.1 us -> 0 us
  between operations: 14.2 us -> 0.68 us
  local copies, waits for them, and re-layouts: 15.6 us -> 5.3 us
    reduce_scatter x1 -> x0, waiting for transfers between devices: 104 us -> none  [body(): lax.psum_scatter(blocks.reshape(span_rows, node_count * 2 * classes), 'ro...]
    psum x2 -> x0, blocking collectives: 102 us -> none  [the longest x1 66 us: body(): node_totals = lax.psum(partial_totals, ('rows', 'feat'))]
    pallas_call x0 -> x1, Pallas kernels: none -> 61.1 us  [body(): pl.pallas_call(kernel, out_shape=(jax.ShapeDtypeStruct((NR, 8, LANES), F3...]
    dot_general x10 -> x0, matrix products: 40.1 us -> none  [the longest x8 38.8 us: one_group(): return jnp.dot(one_hot, flat_weighted, preferred_element_type=jnp.float32)]
    eq x9 -> x0, other arithmetic: 16.3 us -> none  [the longest x8 16.3 us: one_group(): row_bins[None, :, :] == values[:, None, None]]
    all_gather x1 -> x0, blocking collectives: 15.7 us -> none  [body(): grad_all = lax.all_gather(grad_hess, 'feat', axis=0, tiled=True)]
    select_n x15 -> x0, other arithmetic: 13.1 us -> none  [the longest x7 8.49 us: turn(): return jnp.where(position < mine, longer, subtotal)]
    add x10 -> x0, other arithmetic: 8.59 us -> none  [the longest x8 5.17 us: one_group(): values = offset + jnp.arange(bin_group, dtype=jnp.int32)]
  transfers between devices with their start and end apart: 2 -> 0, of which waited for: 1 -> 0; matrix products, arithmetic and copies ran while one was open for 0% -> 0% of each run, Pallas kernels for 0% -> 0%
where the time goes in v1:
time: 67.4 us; the launch traced here: 67.1 us
  Pallas kernels  61.1 us (91%)
  local copies, waits for them, and re-layouts  5.3 us (8%)
  between operations  0.68 us (1%)
    pallas_call x1, Pallas kernels, body(): pl.pallas_call(kernel, out_shape=(jax.ShapeDtypeStruct((NR, 8, LANES), F3...  61.1 us
    unnamed x15, local copies, waits for them, and re-layouts  4.56 us

profile of v1, /device:TPU:1, one launch (start us, length us, event | category | flops | bytes accessed | tf_op | source)
XLA Modules:
  0.0 67.1 jit_solution(17047148538922364939)
XLA Ops:
  0.6 0.0 copy-start.6
  0.6 0.0 copy-start.4
  0.7 0.0 copy-start.5
  0.7 0.6 copy-done.6
  1.3 0.0 copy-done.4
  1.3 0.0 copy-done.5
  1.3 0.0 copy-start
  1.3 1.1 %copy-done = s32[64,3072]{1,0:T(8,128)S(1)} copy-done((s32[64,3072]{1,0:T(8,128)S(1)}, s32[64,3072]{1,0:T(8,128)}, u32[]{:S(2)}) %copy-start) | copy-done | bytes 786456
  2.5 0.0 copy-start.1
  2.5 0.7 %copy-done.1 = s32[3072]{0:T(1024)S(1)} copy-done((s32[3072]{0:T(1024)S(1)}, s32[3072]{0:T(1024)}, u32[]{:S(2)}) %copy-start.1) | copy-done | bytes 12312
  3.2 0.0 copy-start.2
  3.2 0.8 %copy-done.2 = f32[192,32]{0,1:T(8,128)S(1)} copy-done((f32[192,32]{0,1:T(8,128)S(1)}, f32[192,32]{0,1:T(8,128)}, u32[]{:S(2)}) %copy-start.2) | copy-done | bytes 24600
  3.9 0.0 copy-start.3
  3.9 0.7 %copy-done.3 = f32[16,32]{1,0:T(8,128)S(1)} copy-done((f32[16,32]{1,0:T(8,128)S(1)}, f32[16,32]{1,0:T(8,128)}, u32[]{:S(2)}) %copy-start.3) | copy-done | bytes 2072
  4.6 61.1 %shard_map.86 = (f32[8,8,128]{2,1,0:T(8,128)S(1)}, f32[16,64]{1,0:T(8,128)S(1)}) custom-call(s32[8]{0:T(128)S(1)} %copy-done.5, s32[8]{0:T(128)S(1)} %copy-done.6, f32[32,192]{1,0:T(8,128)S(1)} %bitcast.8, s32[1,192]{1,0:T(1,128)S(1)} %bitcast.9, s32[64,3072]{1,0:T(8,128)S(1)} %copy-done, s32[24,128]{1,0:T(8,128)S(1)} %bitcast.6, s32[1,3072]{1,0:T(1,128)S(1)} %bitcast.7, ...), custom_call_target="tpu_custom_call" | custom-call | tf_op jit(solution)/shard_map/pallas_call | solution.py:421
  65.8 0.1 reshape.22
  65.9 0.6 copy.9
  66.5 0.6 copy.11
Async XLA Ops:
  0.6 0.7 copy-start.6
  0.6 0.7 %copy-start.4 = (s32[192]{0:T(256)S(1)}, s32[192]{0:T(256)}, u32[]{:S(2)}) copy-start(s32[192]{0:T(256)} %param.8) | copy-start | bytes 2308
  0.7 0.7 %copy-start.5 = (s32[8]{0:T(128)S(1)}, s32[8]{0:T(128)}, u32[]{:S(2)}) copy-start(s32[8]{0:T(128)} %sf_ref.1) | copy-start | bytes 100
  1.3 1.1 %copy-start = (s32[64,3072]{1,0:T(8,128)S(1)}, s32[64,3072]{1,0:T(8,128)}, u32[]{:S(2)}) copy-start(s32[64,3072]{1,0:T(8,128)} %bins_ref.1) | copy-start | bytes 2359300
  2.5 0.7 %copy-start.1 = (s32[3072]{0:T(1024)S(1)}, s32[3072]{0:T(1024)}, u32[]{:S(2)}) copy-start(s32[3072]{0:T(1024)} %param.10) | copy-start | bytes 36868
  3.2 0.8 %copy-start.2 = (f32[192,32]{0,1:T(8,128)S(1)}, f32[192,32]{0,1:T(8,128)}, u32[]{:S(2)}) copy-start(f32[192,32]{0,1:T(8,128)} %param.7) | copy-start | bytes 73732
  3.9 0.7 %copy-start.3 = (f32[16,32]{1,0:T(8,128)S(1)}, f32[16,32]{1,0:T(8,128)}, u32[]{:S(2)}) copy-start(f32[16,32]{1,0:T(8,128)} %leaf_ref.1) | copy-start | bytes 6148

commit v2 on v1

v2 whole, which is shorter than its diff:
```python
import jax
import jax.numpy as jnp
from jax import lax
from jax.experimental import pallas as pl
from jax.experimental.pallas import tpu as pltpu
from jax.sharding import PartitionSpec as P

MESH = pl.DeviceIdType.MESH
BINS = 64
NODES = 16
CLASSES = 32
COLS = 2 * CLASSES
PARENTS = 8
RIDGE = 1.0
LANES = 128
NR = 8
NF = 16
OWN = 192
GROUP = 3072
KB = GROUP // LANES
FD = 64
FL = FD // NR
FAR_FIRST = (10, 6, 14, 9, 11, 8, 2, 5, 7, 13, 15, 4, 12, 1, 3)
BF = jnp.bfloat16
F32 = jnp.float32


def own_gradients(margins, labels, parents, leaf_t, side):
    leaf = jnp.zeros(margins.shape, F32)
    for p in range(PARENTS):
        column = leaf_t[:, 2 * p + side : 2 * p + side + 1]
        leaf = jnp.where(parents == p, column, leaf)
    logits = margins + leaf
    top = jnp.max(logits, axis=0, keepdims=True)
    grown = jnp.exp(logits - top)
    prob = grown / jnp.sum(grown, axis=0, keepdims=True)
    classes = lax.broadcasted_iota(jnp.int32, margins.shape, 0)
    hot = jnp.where(classes == labels, 1.0, 0.0)
    return prob - hot, 2.0 * prob * (1.0 - prob)


def kernel(
    sf_hbm, sb_hbm, margin_hbm, label_hbm, bins_hbm, par_hbm, parrow_hbm, leaf_hbm,
    gain_ref, total_ref,
    sf_ref, sb_ref, margin_ref, label_ref, bins_ref, par_ref, parrow_ref, leaf_ref,
    bit_f32, bit_send, bit_recv, bin_send, bin_recv, bin_all, node_all,
    spec, grads, acc, unit_tot, gain_send, gain_recv,
    in_sem, bit_ss, bit_rs, bin_ss, bin_rs, node_ss, node_rs, x_ss, x_rs,
    y_ss, y_rs, z_ss, z_rs, far_ss, far_rs, sib_ss, sib_rs, out_ss, out_rs,
):
    row = lax.axis_index("rows")
    feat = lax.axis_index("feat")
    y, core = row // 2, row % 2
    z, x = feat // 4, feat % 4
    odd = feat % 2

    inputs = [
        pltpu.make_async_copy(src, dst, in_sem.at[k])
        for k, (src, dst) in enumerate((
            (bins_hbm, bins_ref), (parrow_hbm, parrow_ref), (sf_hbm, sf_ref),
            (sb_hbm, sb_ref), (margin_hbm, margin_ref), (label_hbm, label_ref),
            (par_hbm, par_ref), (leaf_hbm, leaf_ref),
        ))
    ]
    for copy in inputs:
        copy.start()

    def send(src, dst, ss, rs, r, f):
        return pltpu.make_async_remote_copy(
            src_ref=src, dst_ref=dst, send_sem=ss, recv_sem=rs,
            device_id=(r, f), device_id_type=MESH,
        )

    barrier = pltpu.get_barrier_semaphore()
    for d in FAR_FIRST:
        pl.semaphore_signal(barrier, inc=1, device_id=(row, (feat + d) % NF), device_id_type=MESH)
    for d in range(1, NR):
        pl.semaphore_signal(barrier, inc=1, device_id=((row + d) % NR, feat), device_id_type=MESH)

    for copy in inputs:
        copy.wait()

    right = jnp.zeros((1, GROUP), F32)
    for p in range(PARENTS):
        local = sf_ref[p] - feat * FD
        owned = jnp.logical_and(local >= 0, local < FD).astype(jnp.int32)
        at = jnp.minimum(jnp.maximum(local, 0), FD - 1)
        limit = sb_ref[p] * owned + BINS * (1 - owned)
        hit = jnp.logical_and(bins_ref[pl.ds(at, 1), :] > limit, parrow_ref[...] == p)
        right = jnp.where(hit, 1.0, right)
    bit_f32[...] = jnp.zeros_like(bit_f32)
    for k in range(KB):
        bit_f32[k : k + 1, :] = right[:, k * LANES : (k + 1) * LANES]
    bit_send[...] = bit_f32[...].astype(BF)

    def arrange(value):
        padded = jnp.concatenate(
            [value, jnp.zeros((value.shape[0], 2 * LANES - OWN), value.dtype)], axis=1
        )
        turned = jnp.concatenate([padded[:, 64:], padded[:, :64]], axis=1)
        return jnp.where(odd == 1, turned, padded)

    def rows_of(ref, pair, side):
        main = ref[pl.ds(3 * pair + 2 * side, 1), :]
        rest = ref[pl.ds(3 * pair + 1, 1), :]
        return main, rest

    margins = arrange(margin_ref[...])
    labels = arrange(label_ref[...])
    own_parents = jnp.concatenate(rows_of(par_ref, feat // 2, odd), axis=1)
    leaf_t = leaf_ref[...].T
    first_half = lax.broadcasted_iota(jnp.int32, (CLASSES, LANES), 1) < 64
    keep = first_half == (odd == 0)
    for side in range(2):
        g, h = own_gradients(margins, labels, own_parents, leaf_t, side)
        rest = jnp.where(keep, g[:, LANES:], pltpu.roll(h[:, LANES:], 64, 1))
        spec[x, side] = jnp.concatenate([g[:, :LANES], h[:, :LANES], rest], axis=0).astype(BF)

    def load_bins(to):
        first = pl.multiple_of(to * FL, FL)
        return [
            bins_ref[pl.ds(first, FL), k * LANES : (k + 1) * LANES].astype(F32)
            for k in range(KB)
        ]

    for d in range(1, NR):
        bin_send[d] = jnp.concatenate(load_bins((row + d) % NR), axis=0).astype(BF)
    for k, part in enumerate(load_bins(row)):
        bin_all[row, k] = part

    def bit_copy(d):
        return send(
            bit_send, bit_recv.at[d], bit_ss.at[d], bit_rs.at[d], row, (feat + d) % NF
        )

    def x_copy(d):
        at = spec.at[x]
        return send(at, at, x_ss.at[d], x_rs.at[d], row, 4 * z + (x + d) % 4)

    def bin_copy(d):
        to = (row + d) % NR
        return send(bin_send.at[d], bin_recv.at[d], bin_ss.at[d], bin_rs.at[d], to, feat)

    def node_copy(d):
        to = (row + d) % NR
        return send(node_all.at[row], node_all.at[row], node_ss.at[d], node_rs.at[d], to, feat)

    def arrived(at, sem):
        send(at, at, sem, sem, row, feat).wait_recv()

    def order(i):
        return i + i // 2 - 2 * (i // 3)

    def block(half, dz, dy):
        return grads.at[half, (z + dz) % 4, (y + dy) % 4]

    def y_copy(way):
        at = block(core, 0, 0)
        to = 2 * ((y + 1 + 2 * way) % 4) + core
        return send(at, at, y_ss.at[way], y_rs.at[way], to, feat)

    def y_far_copy(way):
        at = block(core, 0, 3 - 2 * way).at[pl.ds(2 * way, 2)]
        to = 2 * ((y + 1 + 2 * way) % 4) + core
        return send(at, at, y_ss.at[2 + way], y_rs.at[2 + way], to, feat)

    def z_copy(way, i):
        at = block(core, 0, order(i))
        to = 4 * ((z + 1 + 2 * way) % 4) + x
        return send(at, at, z_ss.at[way, i], z_rs.at[way, i], row, to)

    def far_copy(i):
        way = i // 2
        at = block(core, 3 - 2 * way, order(i))
        to = 4 * ((z + 1 + 2 * way) % 4) + x
        return send(at, at, far_ss.at[i], far_rs.at[i], row, to)

    def sib_copy(dz, i):
        at = block(core, dz, order(i))
        return send(at, at, sib_ss.at[dz, i], sib_rs.at[dz, i], row + 1 - 2 * core, feat)

    def sib_wait(dz, i):
        arrived(block(1 - core, dz, order(i)), sib_rs.at[dz, i])

    def pass_on(i):
        sib_copy(0, i).start()
        z_copy(0, i).start()
        z_copy(1, i).start()

    def z_arrival(i):
        for way in range(2):
            arrived(block(core, 3 - 2 * way, order(i)), z_rs.at[way, i])
            if i // 2 == way:
                far_copy(i).start()
            sib_copy(3 - 2 * way, i).start()

    def far_arrival(i):
        arrived(block(core, 2, order(i)), far_rs.at[i])
        sib_copy(2, i).start()

    pl.semaphore_wait(barrier, NF - 1 + NR - 1)
    for d in FAR_FIRST:
        bit_copy(d).start()
    for d in (1, 3, 2):
        x_copy(d).start()
    for d in range(1, NR):
        bin_copy(d).start()

    acc[...] = jnp.zeros_like(acc)

    bits = bit_send[...].astype(F32)
    for d in range(1, NF):
        bit_copy(d).wait_recv()
        bits = bits + bit_recv[d].astype(F32)
    node_all[row] = (2 * par_ref[...]).astype(F32) + bits[:KB]
    bit_f32[...] = bits
    for d in range(1, NR):
        node_copy(d).start()

    for d in (1, 3, 2):
        arrived(spec.at[(x + 4 - d) % 4], x_rs.at[d])
    for xx in range(4):
        main, rest = rows_of(bit_f32, 2 * z + xx // 2, xx % 2)
        low = lax.broadcasted_iota(jnp.int32, (1, LANES), 1) < 64
        turned = jnp.concatenate([rest[:, 64:], rest[:, :64]], axis=1)
        rest = jnp.where(low, rest, turned) if xx % 2 == 0 else jnp.where(low, turned, rest)
        side = jnp.concatenate(
            [jnp.broadcast_to(main, (64, LANES)), jnp.broadcast_to(rest, (32, LANES))], axis=0
        ).astype(BF)
        grads[core, z, y, xx] = jnp.where(side > BF(0.5), spec[xx, 1], spec[xx, 0])
    sib_copy(0, 0).start()
    y_copy(0).start()
    y_copy(1).start()
    z_copy(0, 0).start()
    z_copy(1, 0).start()

    for d in range(1, NR):
        bin_copy(d).wait_recv()
        came = (row + NR - d) % NR
        part = bin_recv[d].astype(F32)
        for k in range(KB):
            bin_all[came, k] = part[k * FL : (k + 1) * FL]
    for d in range(1, NR):
        arrived(node_all.at[(row + NR - d) % NR], node_rs.at[d])

    lane_low = lax.broadcasted_iota(jnp.int32, (32, LANES), 1) < 64
    bin_ids = lax.broadcasted_iota(jnp.int32, (BINS, LANES), 0).astype(F32).astype(BF)
    node_ids = lax.broadcasted_iota(jnp.int32, (NODES, LANES), 0).astype(F32).astype(BF)
    contract = (((1,), (1,)), ((), ()))

    def accumulate(blocks):
        weighted, masks = [], []
        for half, zz, yy in blocks:
            group = 2 * yy + half
            hots, pieces = [], []
            for q in range(2):
                even = grads[half, zz, yy, 2 * q]
                last = grads[half, zz, yy, 2 * q + 1]
                rest_e, rest_o = even[64:], last[64:]
                low = jnp.where(lane_low, rest_e, rest_o)
                high = jnp.where(lane_low, rest_o, rest_e).astype(F32)
                high = pltpu.roll(high, 64, 1).astype(BF)
                middle = jnp.concatenate([low, high], axis=0)
                first = 3 * (2 * zz + q)
                for i, piece in enumerate((even[:64], middle, last[:64])):
                    nodes = node_all[group, pl.ds(first + i, 1), :].astype(BF)
                    wide = jnp.broadcast_to(nodes, (COLS, LANES))
                    zero = jnp.zeros_like(piece)
                    weighted.append(
                        jnp.concatenate(
                            [jnp.where(wide == BF(n), piece, zero) for n in range(NODES)],
                            axis=0,
                        )
                    )
                    same = jnp.broadcast_to(nodes, (NODES, LANES)) == node_ids
                    hots.append(jnp.where(same, BF(1), BF(0)))
                    pieces.append(piece)
                    rows = []
                    for f in range(FL):
                        here = bin_all[group, first + i, f : f + 1, :].astype(BF)
                        under = jnp.broadcast_to(here, (BINS, LANES)) <= bin_ids
                        rows.append(jnp.where(under, BF(1), BF(0)))
                    masks.append(jnp.concatenate(rows, axis=0))
            unit_tot[(half * 4 + zz) * 4 + yy] = lax.dot_general(
                jnp.concatenate(hots, axis=1),
                jnp.concatenate(pieces, axis=1),
                contract,
                preferred_element_type=F32,
            )
        acc[...] += lax.dot_general(
            jnp.concatenate(weighted, axis=1),
            jnp.concatenate(masks, axis=1),
            contract,
            preferred_element_type=F32,
        )

    def near(u, carry):
        @pl.when(u == 0)
        def _():
            sib_wait(0, 0)

        @pl.when(u == 1)
        def _():
            for way in range(2):
                arrived(block(core, 0, 3 - 2 * way), y_rs.at[way])
                y_far_copy(way).start()
            pass_on(1)
            pass_on(2)
            z_arrival(0)

        @pl.when(u == 2)
        def _():
            for way in range(2):
                arrived(block(core, 0, 2).at[pl.ds(2 * way, 2)], y_rs.at[2 + way])
            pass_on(3)
            sib_wait(0, 1)
            sib_wait(0, 2)

        @pl.when(u == 3)
        def _():
            z_arrival(1)
            sib_wait(0, 3)

        mid = ((u + 1) // 2) % 2
        blocks = []
        for j in range(2):
            half = (core + (1 - mid) * j + mid * (u // 2)) % 2
            dy = mid * (1 + 2 * j) + (1 - mid) * 2 * (u // 3)
            blocks.append((half, z, (y + dy) % 4))
        accumulate(blocks)
        return carry

    lax.fori_loop(0, 4, near, 0)

    def beyond(s, carry):
        @pl.when(s == 0)
        def _():
            z_arrival(2)
            sib_wait(3, 0)
            sib_wait(1, 0)

        @pl.when(s == 1)
        def _():
            z_arrival(3)
            sib_wait(3, 1)
            sib_wait(1, 1)

        @pl.when(s == 2)
        def _():
            far_arrival(0)
            far_arrival(1)
            sib_wait(3, 2)
            sib_wait(1, 2)

        @pl.when(s == 3)
        def _():
            far_arrival(2)
            far_arrival(3)
            sib_wait(3, 3)
            sib_wait(1, 3)

        @pl.when(s == 4)
        def _():
            sib_wait(2, 0)
            sib_wait(2, 1)

        @pl.when(s == 5)
        def _():
            sib_wait(2, 2)
            sib_wait(2, 3)

        far = s // 4
        blocks = []
        for j in range(4):
            dz = (1 - far) * (3 - 2 * (j % 2)) + 2 * far
            i = (1 - far) * s + far * (2 * (s - 4) + j % 2)
            blocks.append(((core + j // 2) % 2, (z + dz) % 4, (y + order(i)) % 4))
        accumulate(blocks)
        return carry

    lax.fori_loop(0, 6, beyond, 0)

    for n in range(NODES):
        base = n * COLS
        gl = acc[base : base + CLASSES, :]
        hl = acc[base + CLASSES : base + COLS, :]
        whole_g = acc[base : base + CLASSES, BINS - 1 : BINS]
        whole_h = acc[base + CLASSES : base + COLS, BINS - 1 : BINS]
        gr = whole_g - gl
        hr = whole_h - hl
        score = (
            gl * gl / (hl + RIDGE)
            + gr * gr / (hr + RIDGE)
            - whole_g * whole_g / (whole_h + RIDGE)
        )
        gain = jnp.sum(score, axis=0, keepdims=True) * (1.0 / CLASSES)
        for k in range(4):
            gain_send[n // 2, (n % 2) * 4 + k : (n % 2) * 4 + k + 1, :] = gain[
                :, k * LANES : (k + 1) * LANES
            ]

    def out_copy(d):
        to = (row + d) % NR
        return send(
            gain_send.at[to], gain_recv.at[row], out_ss.at[d], out_rs.at[d], to, feat
        )

    for d in range(1, NR):
        out_copy(d).start()
    gain_ref[row] = gain_send[row]
    for d in range(1, NR):
        came = (row + NR - d) % NR
        at = gain_recv.at[came]
        send(at, at, out_ss.at[d], out_rs.at[d], row, feat).wait_recv()
        gain_ref[came] = gain_recv[came]

    totals = unit_tot[0]
    for u in range(1, 32):
        totals = totals + unit_tot[u]
    total_ref[...] = totals

    for d in range(1, NF):
        bit_copy(d).wait_send()
    for d in range(1, NR):
        bin_copy(d).wait_send()
        node_copy(d).wait_send()
        out_copy(d).wait_send()
    for d in range(1, 4):
        x_copy(d).wait_send()
    for way in range(2):
        y_copy(way).wait_send()
        y_far_copy(way).wait_send()
    for i in range(4):
        z_copy(0, i).wait_send()
        z_copy(1, i).wait_send()
        far_copy(i).wait_send()
        for dz in range(4):
            sib_copy(dz, i).wait_send()


def body(margins, labels, row_bins, parents, split_feature, split_bin, leaf_values):
    vmem = pl.BlockSpec(memory_space=pltpu.VMEM)
    hbm = pl.BlockSpec(memory_space=pltpu.HBM)
    dma = pltpu.SemaphoreType.DMA
    gains, totals = pl.pallas_call(
        kernel,
        out_shape=(
            jax.ShapeDtypeStruct((NR, 8, LANES), F32),
            jax.ShapeDtypeStruct((NODES, COLS), F32),
        ),
        in_specs=[hbm] * 8,
        out_specs=(vmem, vmem),
        scratch_shapes=[
            pltpu.SMEM((PARENTS,), jnp.int32),
            pltpu.SMEM((PARENTS,), jnp.int32),
            pltpu.VMEM((CLASSES, OWN), F32),
            pltpu.VMEM((1, OWN), jnp.int32),
            pltpu.VMEM((FD, GROUP), jnp.int32),
            pltpu.VMEM((KB, LANES), jnp.int32),
            pltpu.VMEM((1, GROUP), jnp.int32),
            pltpu.VMEM((NODES, CLASSES), F32),
            pltpu.VMEM((32, LANES), F32),
            pltpu.VMEM((32, LANES), BF),
            pltpu.VMEM((NF, 32, LANES), BF),
            pltpu.VMEM((NR, KB * FL, LANES), BF),
            pltpu.VMEM((NR, KB * FL, LANES), BF),
            pltpu.VMEM((NR, KB, FL, LANES), F32),
            pltpu.VMEM((NR, KB, LANES), F32),
            pltpu.VMEM((4, 2, 96, LANES), BF),
            pltpu.VMEM((2, 4, 4, 4, 96, LANES), BF),
            pltpu.VMEM((NODES * COLS, FL * BINS), F32),
            pltpu.VMEM((32, NODES, COLS), F32),
            pltpu.VMEM((NR, 8, LANES), F32),
            pltpu.VMEM((NR, 8, LANES), F32),
            dma((8,)),
            dma((NF,)), dma((NF,)), dma((NR,)), dma((NR,)), dma((NR,)), dma((NR,)),
            dma((4,)), dma((4,)), dma((4,)), dma((4,)),
            dma((2, 4)), dma((2, 4)), dma((4,)), dma((4,)), dma((4, 4)), dma((4, 4)),
            dma((NR,)), dma((NR,)),
        ],
        compiler_params=pltpu.CompilerParams(
            collective_id=0, has_side_effects=True, vmem_limit_bytes=58 << 20
        ),
    )(
        split_feature,
        split_bin,
        margins.T,
        labels.reshape(1, OWN),
        row_bins,
        parents.reshape(KB, LANES),
        parents.reshape(1, GROUP),
        leaf_values,
    )
    shaped = gains.reshape(NR, 2, 4, 2, BINS).transpose(1, 0, 2, 3, 4)
    return shaped.reshape(2, FD, BINS), totals


def solution(mesh):
    return jax.shard_map(
        body,
        mesh=mesh,
        in_specs=(
            P(("rows", "feat"), None),
            P(("rows", "feat")),
            P("feat", "rows"),
            P("rows"),
            P(),
            P(),
            P(),
        ),
        out_specs=(P("rows", "feat", None), P()),
        check_vma=False,
    )
```

time: 67.4 us -> 58.8 us (0.87)
  Pallas kernels: 61.1 us -> 55.7 us
  local copies, waits for them, and re-layouts: 5.3 us -> 2.14 us
    pallas_call x1, Pallas kernels: 61.1 us -> 55.7 us  [body(): pl.pallas_call(kernel, out_shape=(jax.ShapeDtypeStruct((NR, 8, LANES), F3...]
    unnamed x15 -> x3, local copies, waits for them, and re-layouts: 4.56 us -> 0.65 us
    reshape x1, local copies, waits for them, and re-layouts: 0.1 us -> 0.85 us  [body(): shaped = gains.reshape(NR, 2, 4, 2, BINS).transpose(1, 0, 2, 3, 4)]
where the time goes in v2:
time: 58.8 us; the launch traced here: 58.5 us
  Pallas kernels  55.7 us (95%)
  local copies, waits for them, and re-layouts  2.14 us (4%)
  between operations  0.66 us (1%)
    pallas_call x1, Pallas kernels, body(): pl.pallas_call(kernel, out_shape=(jax.ShapeDtypeStruct((NR, 8, LANES), F3...  55.7 us

profile of v2, /device:TPU:1, one launch (start us, length us, event | category | flops | bytes accessed | tf_op | source)
XLA Modules:
  0.0 58.5 jit_solution(15247153267528319605)
XLA Ops:
  0.6 55.7 %shard_map.86 = (f32[8,8,128]{2,1,0:T(8,128)}, f32[16,64]{1,0:T(8,128)}) custom-call(s32[8]{0:T(128)} %sf_hbm.1, s32[8]{0:T(128)} %sb_hbm.1, f32[32,192]{1,0:T(8,128)} %bitcast.10, s32[1,192]{1,0:T(1,128)} %bitcast.11, s32[64,3072]{1,0:T(8,128)} %bins_hbm.1, s32[24,128]{1,0:T(8,128)} %bitcast.8, s32[1,3072]{1,0:T(1,128)} %bitcast.9, f32[16,32]{1,0:T(8,128)} %leaf_hbm.1), custom_call_target="tpu_custom_call" | custom-call | tf_op jit(solution)/shard_map/pallas_call | solution.py:445
  56.4 0.9 %reshape.22 = f32[8,2,4,2,64]{4,3,2,1,0:T(2,128)S(1)} reshape(f32[8,8,128]{2,1,0:T(8,128)} %get-tuple-element.4) | data formatting | bytes 65536 | tf_op jit(solution)/shard_map/reshape | solution.py:494
  57.2 0.0 copy-start
  57.2 0.6 %copy.9 = f32[2,8,4,2,64]{4,3,2,1,0:T(2,128)} copy(f32[2,8,4,2,64]{4,3,2,0,1:T(2,128)S(1)} %bitcast.6) | data formatting | bytes 65536 | tf_op jit(solution)/shard_map/transpose | solution.py:494
  57.9 0.1 copy-done
  57.9 0.6 %copy.11 = f32[16,64]{1,0:T(8,128)} copy(f32[16,64]{1,0:T(8,128)S(1)} %copy-done) | data formatting | bytes 8192
Async XLA Ops:
  57.2 0.7 %copy-start = (f32[16,64]{1,0:T(8,128)S(1)}, f32[16,64]{1,0:T(8,128)}, u32[]{:S(2)}) copy-start(f32[16,64]{1,0:T(8,128)} %get-tuple-element.9) | copy-start | bytes 12292

commit v3 on v2

--- a/solution.py
+++ b/solution.py
@@ -21,6 +21,8 @@
 FD = 64
 FL = FD // NR
 FAR_FIRST = (10, 6, 14, 9, 11, 8, 2, 5, 7, 13, 15, 4, 12, 1, 3)
+ROW_ORDER = ((0, 1), (1, 0), (1, 1), (3, 0), (3, 1), (2, 0), (2, 1))
+FAR_ROWS = (5, 6, 1, 2, 3, 4, 0)
 BF = jnp.bfloat16
 F32 = jnp.float32
 
@@ -46,13 +48,25 @@
     bit_f32, bit_send, bit_recv, bin_send, bin_recv, bin_all, node_all,
     spec, grads, acc, unit_tot, gain_send, gain_recv,
     in_sem, bit_ss, bit_rs, bin_ss, bin_rs, node_ss, node_rs, x_ss, x_rs,
-    y_ss, y_rs, z_ss, z_rs, far_ss, far_rs, sib_ss, sib_rs, out_ss, out_rs,
+    z_ss, z_rs, y_ss, y_rs, far_ss, far_rs, sib_ss, sib_rs, out_ss, out_rs,
 ):
     row = lax.axis_index("rows")
     feat = lax.axis_index("feat")
     y, core = row // 2, row % 2
     z, x = feat // 4, feat % 4
     odd = feat % 2
+
+    def send(src, dst, ss, rs, r, f):
+        return pltpu.make_async_remote_copy(
+            src_ref=src, dst_ref=dst, send_sem=ss, recv_sem=rs,
+            device_id=(r, f), device_id_type=MESH,
+        )
+
+    barrier = pltpu.get_barrier_semaphore()
+    for d in FAR_FIRST:
+        pl.semaphore_signal(barrier, inc=1, device_id=(row, (feat + d) % NF), device_id_type=MESH)
+    for d in range(1, NR):
+        pl.semaphore_signal(barrier, inc=1, device_id=((row + d) % NR, feat), device_id_type=MESH)
 
     inputs = [
         pltpu.make_async_copy(src, dst, in_sem.at[k])
@@ -64,19 +78,6 @@
     ]
     for copy in inputs:
         copy.start()
-
-    def send(src, dst, ss, rs, r, f):
-        return pltpu.make_async_remote_copy(
-            src_ref=src, dst_ref=dst, send_sem=ss, recv_sem=rs,
-            device_id=(r, f), device_id_type=MESH,
-        )
-
-    barrier = pltpu.get_barrier_semaphore()
-    for d in FAR_FIRST:
-        pl.semaphore_signal(barrier, inc=1, device_id=(row, (feat + d) % NF), device_id_type=MESH)
-    for d in range(1, NR):
-        pl.semaphore_signal(barrier, inc=1, device_id=((row + d) % NR, feat), device_id_type=MESH)
-
     for copy in inputs:
         copy.wait()
 
@@ -123,8 +124,11 @@
             for k in range(KB)
         ]
 
-    for d in range(1, NR):
-        bin_send[d] = jnp.concatenate(load_bins((row + d) % NR), axis=0).astype(BF)
+    def row_at(dy, other):
+        return 2 * ((y + dy) % 4) + (core + other) % 2
+
+    for d, (dy, other) in enumerate(ROW_ORDER):
+        bin_send[d] = jnp.concatenate(load_bins(row_at(dy, other)), axis=0).astype(BF)
     for k, part in enumerate(load_bins(row)):
         bin_all[row, k] = part
 
@@ -138,11 +142,11 @@
         return send(at, at, x_ss.at[d], x_rs.at[d], row, 4 * z + (x + d) % 4)
 
     def bin_copy(d):
-        to = (row + d) % NR
+        to = row_at(*ROW_ORDER[d])
         return send(bin_send.at[d], bin_recv.at[d], bin_ss.at[d], bin_rs.at[d], to, feat)
 
     def node_copy(d):
-        to = (row + d) % NR
+        to = row_at(*ROW_ORDER[d])
         return send(node_all.at[row], node_all.at[row], node_ss.at[d], node_rs.at[d], to, feat)
 
     def arrived(at, sem):
@@ -154,56 +158,63 @@
     def block(half, dz, dy):
         return grads.at[half, (z + dz) % 4, (y + dy) % 4]
 
-    def y_copy(way):
+    def z_copy(way):
         at = block(core, 0, 0)
-        to = 2 * ((y + 1 + 2 * way) % 4) + core
-        return send(at, at, y_ss.at[way], y_rs.at[way], to, feat)
-
-    def y_far_copy(way):
-        at = block(core, 0, 3 - 2 * way).at[pl.ds(2 * way, 2)]
-        to = 2 * ((y + 1 + 2 * way) % 4) + core
-        return send(at, at, y_ss.at[2 + way], y_rs.at[2 + way], to, feat)
-
-    def z_copy(way, i):
-        at = block(core, 0, order(i))
         to = 4 * ((z + 1 + 2 * way) % 4) + x
-        return send(at, at, z_ss.at[way, i], z_rs.at[way, i], row, to)
-
-    def far_copy(i):
+        return send(at, at, z_ss.at[way], z_rs.at[way], row, to)
+
+    def z_far_copy(way):
+        at = block(core, 3 - 2 * way, 0).at[pl.ds(2 * way, 2)]
+        to = 4 * ((z + 1 + 2 * way) % 4) + x
+        return send(at, at, z_ss.at[2 + way], z_rs.at[2 + way], row, to)
+
+    def y_copy(way, i):
+        at = block(core, order(i), 0)
+        return send(at, at, y_ss.at[way, i], y_rs.at[way, i], row_at(1 + 2 * way, 0), feat)
+
+    def y_far_copy(i):
         way = i // 2
-        at = block(core, 3 - 2 * way, order(i))
-        to = 4 * ((z + 1 + 2 * way) % 4) + x
-        return send(at, at, far_ss.at[i], far_rs.at[i], row, to)
-
-    def sib_copy(dz, i):
-        at = block(core, dz, order(i))
-        return send(at, at, sib_ss.at[dz, i], sib_rs.at[dz, i], row + 1 - 2 * core, feat)
-
-    def sib_wait(dz, i):
-        arrived(block(1 - core, dz, order(i)), sib_rs.at[dz, i])
+        at = block(core, order(i), 3 - 2 * way)
+        return send(at, at, far_ss.at[i], far_rs.at[i], row_at(1 + 2 * way, 0), feat)
+
+    def sib_copy(dy, i):
+        at = block(core, order(i), dy)
+        return send(at, at, sib_ss.at[dy, i], sib_rs.at[dy, i], row_at(0, 1), feat)
+
+    def sib_wait(dy, i):
+        arrived(block(1 - core, order(i), dy), sib_rs.at[dy, i])
 
     def pass_on(i):
         sib_copy(0, i).start()
-        z_copy(0, i).start()
-        z_copy(1, i).start()
-
-    def z_arrival(i):
+        y_copy(0, i).start()
+        y_copy(1, i).start()
+
+    def y_arrival(i):
         for way in range(2):
-            arrived(block(core, 3 - 2 * way, order(i)), z_rs.at[way, i])
+            arrived(block(core, order(i), 3 - 2 * way), y_rs.at[way, i])
             if i // 2 == way:
-                far_copy(i).start()
+                y_far_copy(i).start()
             sib_copy(3 - 2 * way, i).start()
 
     def far_arrival(i):
-        arrived(block(core, 2, order(i)), far_rs.at[i])
+        arrived(block(core, order(i), 2), far_rs.at[i])
         sib_copy(2, i).start()
+
+    def row_arrival(d):
+        bin_copy(d).wait_recv()
+        dy, other = ROW_ORDER[d]
+        came = row_at(4 - dy, other)
+        part = bin_recv[d].astype(F32)
+        for k in range(KB):
+            bin_all[came, k] = part[k * FL : (k + 1) * FL]
+        arrived(node_all.at[came], node_rs.at[d])
 
     pl.semaphore_wait(barrier, NF - 1 + NR - 1)
     for d in FAR_FIRST:
         bit_copy(d).start()
     for d in (1, 3, 2):
         x_copy(d).start()
-    for d in range(1, NR):
+    for d in range(NR - 1):
         bin_copy(d).start()
 
     acc[...] = jnp.zeros_like(acc)
@@ -214,7 +225,7 @@
         bits = bits + bit_recv[d].astype(F32)
     node_all[row] = (2 * par_ref[...]).astype(F32) + bits[:KB]
     bit_f32[...] = bits
-    for d in range(1, NR):
+    for d in range(NR - 1):
         node_copy(d).start()
 
     for d in (1, 3, 2):
@@ -229,19 +240,11 @@
         ).astype(BF)
         grads[core, z, y, xx] = jnp.where(side > BF(0.5), spec[xx, 1], spec[xx, 0])
     sib_copy(0, 0).start()
-    y_copy(0).start()
-    y_copy(1).start()
-    z_copy(0, 0).start()
-    z_copy(1, 0).start()
-
-    for d in range(1, NR):
-        bin_copy(d).wait_recv()
-        came = (row + NR - d) % NR
-        part = bin_recv[d].astype(F32)
-        for k in range(KB):
-            bin_all[came, k] = part[k * FL : (k + 1) * FL]
-    for d in range(1, NR):
-        arrived(node_all.at[(row + NR - d) % NR], node_rs.at[d])
+    z_copy(0).start()
+    z_copy(1).start()
+    y_copy(0, 0).start()
+    y_copy(1, 0).start()
+    row_arrival(0)
 
     lane_low = lax.broadcasted_iota(jnp.int32, (32, LANES), 1) < 64
     bin_ids = lax.broadcasted_iota(jnp.int32, (BINS, LANES), 0).astype(F32).astype(BF)
@@ -294,59 +297,68 @@
             preferred_element_type=F32,
         )
 
+    def first(u, carry):
+        @pl.when(u == 1)
+        def _():
+            sib_wait(0, 0)
+
+        accumulate([((core + u) % 2, z, y)])
+        return carry
+
+    lax.fori_loop(0, 2, first, 0)
+
     def near(u, carry):
         @pl.when(u == 0)
         def _():
-            sib_wait(0, 0)
-
-        @pl.when(u == 1)
-        def _():
             for way in range(2):
-                arrived(block(core, 0, 3 - 2 * way), y_rs.at[way])
-                y_far_copy(way).start()
+                arrived(block(core, 3 - 2 * way, 0), z_rs.at[way])
+                z_far_copy(way).start()
             pass_on(1)
             pass_on(2)
-            z_arrival(0)
-
-        @pl.when(u == 2)
-        def _():
-            for way in range(2):
-                arrived(block(core, 0, 2).at[pl.ds(2 * way, 2)], y_rs.at[2 + way])
-            pass_on(3)
+
+        @pl.when(u == 1)
+        def _():
             sib_wait(0, 1)
             sib_wait(0, 2)
 
-        @pl.when(u == 3)
-        def _():
-            z_arrival(1)
+        @pl.when(u == 2)
+        def _():
+            for way in range(2):
+                arrived(block(core, 2, 0).at[pl.ds(2 * way, 2)], z_rs.at[2 + way])
+            pass_on(3)
+            y_arrival(0)
             sib_wait(0, 3)
 
-        mid = ((u + 1) // 2) % 2
+        last = u // 2
         blocks = []
         for j in range(2):
-            half = (core + (1 - mid) * j + mid * (u // 2)) % 2
-            dy = mid * (1 + 2 * j) + (1 - mid) * 2 * (u // 3)
-            blocks.append((half, z, (y + dy) % 4))
+            half = (core + (1 - last) * u + last * j) % 2
+            dz = (1 - last) * (1 + 2 * j) + 2 * last
+            blocks.append((half, (z + dz) % 4, y))
         accumulate(blocks)
         return carry
 
-    lax.fori_loop(0, 4, near, 0)
+    lax.fori_loop(0, 3, near, 0)
+
+    for d in range(1, NR - 1):
+        row_arrival(d)
 
     def beyond(s, carry):
         @pl.when(s == 0)
         def _():
-            z_arrival(2)
+            y_arrival(1)
             sib_wait(3, 0)
             sib_wait(1, 0)
 
         @pl.when(s == 1)
         def _():
-            z_arrival(3)
+            y_arrival(2)
             sib_wait(3, 1)
             sib_wait(1, 1)
 
         @pl.when(s == 2)
         def _():
+            y_arrival(3)
             far_arrival(0)
             far_arrival(1)
             sib_wait(3, 2)
@@ -372,9 +384,9 @@
         far = s // 4
         blocks = []
         for j in range(4):
-            dz = (1 - far) * (3 - 2 * (j % 2)) + 2 * far
+            dy = (1 - far) * (3 - 2 * (j % 2)) + 2 * far
             i = (1 - far) * s + far * (2 * (s - 4) + j % 2)
-            blocks.append(((core + j // 2) % 2, (z + dz) % 4, (y + order(i)) % 4))
+            blocks.append(((core + j // 2) % 2, (z + order(i)) % 4, (y + dy) % 4))
         accumulate(blocks)
         return carry
 
@@ -394,58 +406,56 @@
             - whole_g * whole_g / (whole_h + RIDGE)
         )
         gain = jnp.sum(score, axis=0, keepdims=True) * (1.0 / CLASSES)
-        for k in range(4):
-            gain_send[n // 2, (n % 2) * 4 + k : (n % 2) * 4 + k + 1, :] = gain[
-                :, k * LANES : (k + 1) * LANES
-            ]
+        for f in range(FL):
+            gain_send[n // 2, n % 2, f : f + 1, :] = gain[:, f * BINS : (f + 1) * BINS]
+
+    def gain_at(r):
+        return gain_recv.at[:, pl.ds(pl.multiple_of(r * FL, FL), FL)]
 
     def out_copy(d):
-        to = (row + d) % NR
-        return send(
-            gain_send.at[to], gain_recv.at[row], out_ss.at[d], out_rs.at[d], to, feat
-        )
-
-    for d in range(1, NR):
+        to = row_at(*ROW_ORDER[d])
+        return send(gain_send.at[to], gain_at(row), out_ss.at[d], out_rs.at[d], to, feat)
+
+    for d in FAR_ROWS:
         out_copy(d).start()
-    gain_ref[row] = gain_send[row]
-    for d in range(1, NR):
-        came = (row + NR - d) % NR
-        at = gain_recv.at[came]
-        send(at, at, out_ss.at[d], out_rs.at[d], row, feat).wait_recv()
-        gain_ref[came] = gain_recv[came]
-
+    for n in range(2):
+        gain_recv[n, pl.ds(pl.multiple_of(row * FL, FL), FL)] = gain_send[row, n]
     totals = unit_tot[0]
     for u in range(1, 32):
         totals = totals + unit_tot[u]
     total_ref[...] = totals
+    for d in range(NR - 1):
+        dy, other = ROW_ORDER[d]
+        arrived(gain_at(row_at(4 - dy, other)), out_rs.at[d])
+    gain_ref[...] = gain_recv[...]
 
     for d in range(1, NF):
         bit_copy(d).wait_send()
-    for d in range(1, NR):
+    for d in range(NR - 1):
         bin_copy(d).wait_send()
         node_copy(d).wait_send()
         out_copy(d).wait_send()
     for d in range(1, 4):
         x_copy(d).wait_send()
     for way in range(2):
-        y_copy(way).wait_send()
-        y_far_copy(way).wait_send()
+        z_copy(way).wait_send()
+        z_far_copy(way).wait_send()
     for i in range(4):
-        z_copy(0, i).wait_send()
-        z_copy(1, i).wait_send()
-        far_copy(i).wait_send()
-        for dz in range(4):
-            sib_copy(dz, i).wait_send()
+        y_copy(0, i).wait_send()
+        y_copy(1, i).wait_send()
+        y_far_copy(i).wait_send()
+        for dy in range(4):
+            sib_copy(dy, i).wait_send()
 
 
 def body(margins, labels, row_bins, parents, split_feature, split_bin, leaf_values):
     vmem = pl.BlockSpec(memory_space=pltpu.VMEM)
     hbm = pl.BlockSpec(memory_space=pltpu.HBM)
     dma = pltpu.SemaphoreType.DMA
-    gains, totals = pl.pallas_call(
+    return pl.pallas_call(
         kernel,
         out_shape=(
-            jax.ShapeDtypeStruct((NR, 8, LANES), F32),
+            jax.ShapeDtypeStruct((2, FD, BINS), F32),
             jax.ShapeDtypeStruct((NODES, COLS), F32),
         ),
         in_specs=[hbm] * 8,
@@ -470,8 +480,8 @@
             pltpu.VMEM((2, 4, 4, 4, 96, LANES), BF),
             pltpu.VMEM((NODES * COLS, FL * BINS), F32),
             pltpu.VMEM((32, NODES, COLS), F32),
-            pltpu.VMEM((NR, 8, LANES), F32),
-            pltpu.VMEM((NR, 8, LANES), F32),
+            pltpu.VMEM((NR, 2, FL, BINS), F32),
+            pltpu.VMEM((2, FD, BINS), F32),
             dma((8,)),
             dma((NF,)), dma((NF,)), dma((NR,)), dma((NR,)), dma((NR,)), dma((NR,)),
             dma((4,)), dma((4,)), dma((4,)), dma((4,)),
@@ -491,8 +501,6 @@
         parents.reshape(1, GROUP),
         leaf_values,
     )
-    shaped = gains.reshape(NR, 2, 4, 2, BINS).transpose(1, 0, 2, 3, 4)
-    return shaped.reshape(2, FD, BINS), totals
 
 
 def solution(mesh):

time: 58.8 us -> 58.2 us (0.990)
    unnamed x3 -> x4, local copies, waits for them, and re-layouts: 0.65 us -> 2.08 us
    reshape x1 -> x0, local copies, waits for them, and re-layouts: 0.85 us -> none  [body(): shaped = gains.reshape(NR, 2, 4, 2, BINS).transpose(1, 0, 2, 3, 4)]
    transpose x1 -> x0, local copies, waits for them, and re-layouts: 0.63 us -> none  [body(): shaped = gains.reshape(NR, 2, 4, 2, BINS).transpose(1, 0, 2, 3, 4)]
where the time goes in v3:
time: 58.2 us; the launch traced here: 58 us
  Pallas kernels  55.3 us (95%)
  local copies, waits for them, and re-layouts  2.08 us (4%)
  between operations  0.65 us (1%)
    pallas_call x1, Pallas kernels, body(): pl.pallas_call(kernel, out_shape=(jax.ShapeDtypeStruct((2, FD, BINS), F32...  55.3 us
    unnamed x4, local copies, waits for them, and re-layouts  2.08 us

profile of v3, /device:TPU:1, one launch (start us, length us, event | category | flops | bytes accessed | tf_op | source)
XLA Modules:
  0.0 58.0 jit_solution(13875482617133243757)
XLA Ops:
  0.6 55.3 %shard_map.86 = (f32[2,64,64]{2,1,0:T(8,128)}, f32[16,64]{1,0:T(8,128)}) custom-call(s32[8]{0:T(128)} %sf_hbm.1, s32[8]{0:T(128)} %sb_hbm.1, f32[32,192]{1,0:T(8,128)} %bitcast.6, s32[1,192]{1,0:T(1,128)} %bitcast.7, s32[64,3072]{1,0:T(8,128)} %bins_hbm.1, s32[24,128]{1,0:T(8,128)} %bitcast.4, s32[1,3072]{1,0:T(1,128)} %bitcast.5, f32[16,32]{1,0:T(8,128)} %leaf_hbm.1), custom_call_target="tpu_custom_call" | custom-call | tf_op jit(solution)/shard_map/pallas_call | solution.py:455
  55.9 0.0 copy-start
  55.9 1.5 %copy.11 = f32[2,64,64]{2,1,0:T(8,128)} copy(f32[2,64,64]{2,1,0:T(8,128)} %get-tuple-element.4) | data formatting | bytes 65536
  57.4 0.0 copy-done
  57.4 0.6 %copy.12 = f32[16,64]{1,0:T(8,128)} copy(f32[16,64]{1,0:T(8,128)S(1)} %copy-done) | data formatting | bytes 8192
Async XLA Ops:
  55.9 1.5 %copy-start = (f32[16,64]{1,0:T(8,128)S(1)}, f32[16,64]{1,0:T(8,128)}, u32[]{:S(2)}) copy-start(f32[16,64]{1,0:T(8,128)} %get-tuple-element.5) | copy-start | bytes 12292

commit v4 on v3

--- a/solution.py
+++ b/solution.py
@@ -46,9 +46,10 @@
     gain_ref, total_ref,
     sf_ref, sb_ref, margin_ref, label_ref, bins_ref, par_ref, parrow_ref, leaf_ref,
     bit_f32, bit_send, bit_recv, bin_send, bin_recv, bin_all, node_all,
-    spec, grads, acc, unit_tot, gain_send, gain_recv,
+    spec, grads, acc, chunk_tot, group_tot, gain_send, gain_recv,
     in_sem, bit_ss, bit_rs, bin_ss, bin_rs, node_ss, node_rs, x_ss, x_rs,
     z_ss, z_rs, y_ss, y_rs, far_ss, far_rs, sib_ss, sib_rs, out_ss, out_rs,
+    ct_ss, ct_rs, gt_ss, gt_rs,
 ):
     row = lax.axis_index("rows")
     feat = lax.axis_index("feat")
@@ -127,11 +128,6 @@
     def row_at(dy, other):
         return 2 * ((y + dy) % 4) + (core + other) % 2
 
-    for d, (dy, other) in enumerate(ROW_ORDER):
-        bin_send[d] = jnp.concatenate(load_bins(row_at(dy, other)), axis=0).astype(BF)
-    for k, part in enumerate(load_bins(row)):
-        bin_all[row, k] = part
-
     def bit_copy(d):
         return send(
             bit_send, bit_recv.at[d], bit_ss.at[d], bit_rs.at[d], row, (feat + d) % NF
@@ -214,8 +210,11 @@
         bit_copy(d).start()
     for d in (1, 3, 2):
         x_copy(d).start()
-    for d in range(NR - 1):
+    for d, (dy, other) in enumerate(ROW_ORDER):
+        bin_send[d] = jnp.concatenate(load_bins(row_at(dy, other)), axis=0).astype(BF)
         bin_copy(d).start()
+    for k, part in enumerate(load_bins(row)):
+        bin_all[row, k] = part
 
     acc[...] = jnp.zeros_like(acc)
 
@@ -251,21 +250,22 @@
     node_ids = lax.broadcasted_iota(jnp.int32, (NODES, LANES), 0).astype(F32).astype(BF)
     contract = (((1,), (1,)), ((), ()))
 
+    def pair_pieces(half, zz, yy, q):
+        even = grads[half, zz, yy, 2 * q]
+        last = grads[half, zz, yy, 2 * q + 1]
+        rest_e, rest_o = even[64:], last[64:]
+        low = jnp.where(lane_low, rest_e, rest_o)
+        high = jnp.where(lane_low, rest_o, rest_e).astype(F32)
+        high = pltpu.roll(high, 64, 1).astype(BF)
+        return even[:64], jnp.concatenate([low, high], axis=0), last[:64]
+
     def accumulate(blocks):
         weighted, masks = [], []
         for half, zz, yy in blocks:
             group = 2 * yy + half
-            hots, pieces = [], []
             for q in range(2):
-                even = grads[half, zz, yy, 2 * q]
-                last = grads[half, zz, yy, 2 * q + 1]
-                rest_e, rest_o = even[64:], last[64:]
-                low = jnp.where(lane_low, rest_e, rest_o)
-                high = jnp.where(lane_low, rest_o, rest_e).astype(F32)
-                high = pltpu.roll(high, 64, 1).astype(BF)
-                middle = jnp.concatenate([low, high], axis=0)
                 first = 3 * (2 * zz + q)
-                for i, piece in enumerate((even[:64], middle, last[:64])):
+                for i, piece in enumerate(pair_pieces(half, zz, yy, q)):
                     nodes = node_all[group, pl.ds(first + i, 1), :].astype(BF)
                     wide = jnp.broadcast_to(nodes, (COLS, LANES))
                     zero = jnp.zeros_like(piece)
@@ -275,21 +275,12 @@
                             axis=0,
                         )
                     )
-                    same = jnp.broadcast_to(nodes, (NODES, LANES)) == node_ids
-                    hots.append(jnp.where(same, BF(1), BF(0)))
-                    pieces.append(piece)
                     rows = []
                     for f in range(FL):
                         here = bin_all[group, first + i, f : f + 1, :].astype(BF)
                         under = jnp.broadcast_to(here, (BINS, LANES)) <= bin_ids
                         rows.append(jnp.where(under, BF(1), BF(0)))
                     masks.append(jnp.concatenate(rows, axis=0))
-            unit_tot[(half * 4 + zz) * 4 + yy] = lax.dot_general(
-                jnp.concatenate(hots, axis=1),
-                jnp.concatenate(pieces, axis=1),
-                contract,
-                preferred_element_type=F32,
-            )
         acc[...] += lax.dot_general(
             jnp.concatenate(weighted, axis=1),
             jnp.concatenate(masks, axis=1),
@@ -297,6 +288,31 @@
             preferred_element_type=F32,
         )
 
+    hots, pieces = [], []
+    for q in range(2):
+        for i, piece in enumerate(pair_pieces(core, z, y, q)):
+            nodes = node_all[row, pl.ds(3 * (2 * z + q) + i, 1), :].astype(BF)
+            same = jnp.broadcast_to(nodes, (NODES, LANES)) == node_ids
+            hots.append(jnp.where(same, BF(1), BF(0)))
+            pieces.append(piece)
+    chunk_tot[z] = lax.dot_general(
+        jnp.concatenate(hots, axis=1),
+        jnp.concatenate(pieces, axis=1),
+        contract,
+        preferred_element_type=F32,
+    )
+
+    def chunk_tot_copy(d):
+        at = chunk_tot.at[z]
+        return send(at, at, ct_ss.at[d], ct_rs.at[d], row, 4 * ((z + d) % 4) + x)
+
+    def group_tot_copy(d):
+        at = group_tot.at[row]
+        return send(at, at, gt_ss.at[d], gt_rs.at[d], row_at(*ROW_ORDER[d]), feat)
+
+    for d in range(1, 4):
+        chunk_tot_copy(d).start()
+
     def first(u, carry):
         @pl.when(u == 1)
         def _():
@@ -321,27 +337,25 @@
             sib_wait(0, 1)
             sib_wait(0, 2)
 
-        @pl.when(u == 2)
-        def _():
-            for way in range(2):
-                arrived(block(core, 2, 0).at[pl.ds(2 * way, 2)], z_rs.at[2 + way])
-            pass_on(3)
-            y_arrival(0)
-            sib_wait(0, 3)
-
-        last = u // 2
-        blocks = []
-        for j in range(2):
-            half = (core + (1 - last) * u + last * j) % 2
-            dz = (1 - last) * (1 + 2 * j) + 2 * last
-            blocks.append((half, (z + dz) % 4, y))
-        accumulate(blocks)
+        half = (core + u) % 2
+        accumulate([(half, (z + 1) % 4, y), (half, (z + 3) % 4, y)])
         return carry
 
-    lax.fori_loop(0, 3, near, 0)
+    lax.fori_loop(0, 2, near, 0)
+
+    for way in range(2):
+        arrived(block(core, 2, 0).at[pl.ds(2 * way, 2)], z_rs.at[2 + way])
+    pass_on(3)
+    y_arrival(0)
 
     for d in range(1, NR - 1):
         row_arrival(d)
+
+    for d in range(1, 4):
+        arrived(chunk_tot.at[(z + 4 - d) % 4], ct_rs.at[d])
+    group_tot[row] = (chunk_tot[0] + chunk_tot[1]) + (chunk_tot[2] + chunk_tot[3])
+    for d in range(NR - 1):
+        group_tot_copy(d).start()
 
     def beyond(s, carry):
         @pl.when(s == 0)
@@ -391,6 +405,9 @@
         return carry
 
     lax.fori_loop(0, 6, beyond, 0)
+
+    sib_wait(0, 3)
+    accumulate([(core, (z + 2) % 4, y), (1 - core, (z + 2) % 4, y)])
 
     for n in range(NODES):
         base = n * COLS
@@ -406,28 +423,34 @@
             - whole_g * whole_g / (whole_h + RIDGE)
         )
         gain = jnp.sum(score, axis=0, keepdims=True) * (1.0 / CLASSES)
-        for f in range(FL):
-            gain_send[n // 2, n % 2, f : f + 1, :] = gain[:, f * BINS : (f + 1) * BINS]
-
-    def gain_at(r):
-        return gain_recv.at[:, pl.ds(pl.multiple_of(r * FL, FL), FL)]
+        for k in range(4):
+            at = (n % 2) * 4 + k
+            gain_send[n // 2, at : at + 1, :] = gain[:, k * LANES : (k + 1) * LANES]
 
     def out_copy(d):
         to = row_at(*ROW_ORDER[d])
-        return send(gain_send.at[to], gain_at(row), out_ss.at[d], out_rs.at[d], to, feat)
+        return send(gain_send.at[to], gain_recv.at[row], out_ss.at[d], out_rs.at[d], to, feat)
 
     for d in FAR_ROWS:
         out_copy(d).start()
-    for n in range(2):
-        gain_recv[n, pl.ds(pl.multiple_of(row * FL, FL), FL)] = gain_send[row, n]
-    totals = unit_tot[0]
-    for u in range(1, 32):
-        totals = totals + unit_tot[u]
-    total_ref[...] = totals
+    gain_recv[row] = gain_send[row]
     for d in range(NR - 1):
         dy, other = ROW_ORDER[d]
-        arrived(gain_at(row_at(4 - dy, other)), out_rs.at[d])
-    gain_ref[...] = gain_recv[...]
+        arrived(group_tot.at[row_at(4 - dy, other)], gt_rs.at[d])
+    totals = group_tot[0]
+    for r in range(1, NR):
+        totals = totals + group_tot[r]
+    total_ref[...] = totals
+
+    for d in range(NR - 1):
+        dy, other = ROW_ORDER[d]
+        arrived(gain_recv.at[row_at(4 - dy, other)], out_rs.at[d])
+    for r in range(NR):
+        for n in range(2):
+            tile = gain_recv[r, 4 * n : 4 * n + 4, :]
+            for side in range(2):
+                at = pl.ds(r * FL + side, 4, stride=2)
+                gain_ref[n, at, :] = tile[:, side * BINS : (side + 1) * BINS]
 
     for d in range(1, NF):
         bit_copy(d).wait_send()
@@ -435,8 +458,10 @@
         bin_copy(d).wait_send()
         node_copy(d).wait_send()
         out_copy(d).wait_send()
+        group_tot_copy(d).wait_send()
     for d in range(1, 4):
         x_copy(d).wait_send()
+        chunk_tot_copy(d).wait_send()
     for way in range(2):
         z_copy(way).wait_send()
         z_far_copy(way).wait_send()
@@ -479,27 +504,34 @@
             pltpu.VMEM((4, 2, 96, LANES), BF),
             pltpu.VMEM((2, 4, 4, 4, 96, LANES), BF),
             pltpu.VMEM((NODES * COLS, FL * BINS), F32),
-            pltpu.VMEM((32, NODES, COLS), F32),
-            pltpu.VMEM((NR, 2, FL, BINS), F32),
-            pltpu.VMEM((2, FD, BINS), F32),
+            pltpu.VMEM((4, NODES, COLS), F32),
+            pltpu.VMEM((NR, NODES, COLS), F32),
+            pltpu.VMEM((NR, 8, LANES), F32),
+            pltpu.VMEM((NR, 8, LANES), F32),
             dma((8,)),
             dma((NF,)), dma((NF,)), dma((NR,)), dma((NR,)), dma((NR,)), dma((NR,)),
             dma((4,)), dma((4,)), dma((4,)), dma((4,)),
             dma((2, 4)), dma((2, 4)), dma((4,)), dma((4,)), dma((4, 4)), dma((4, 4)),
             dma((NR,)), dma((NR,)),
+            dma((4,)), dma((4,)), dma((NR,)), dma((NR,)),
         ],
         compiler_params=pltpu.CompilerParams(
-            collective_id=0, has_side_effects=True, vmem_limit_bytes=58 << 20
+            collective_id=0, has_side_effects=True, vmem_limit_bytes=48 << 20
         ),
     )(
-        split_feature,
-        split_bin,
-        margins.T,
-        labels.reshape(1, OWN),
-        row_bins,
-        parents.reshape(KB, LANES),
-        parents.reshape(1, GROUP),
-        leaf_values,
+        *(
+            pltpu.with_memory_space_constraint(value, pltpu.HBM)
+            for value in (
+                split_feature,
+                split_bin,
+                margins.T,
+                labels.reshape(1, OWN),
+                row_bins,
+                parents.reshape(KB, LANES),
+                parents.reshape(1, GROUP),
+                leaf_values,
+            )
+        )
     )
 
 

time: 58.2 us -> 55.5 us (0.954)
  Pallas kernels: 55.3 us -> 53.5 us
  local copies, waits for them, and re-layouts: 2.08 us -> 1.23 us
    pallas_call x1, Pallas kernels: 55.3 us -> 53.5 us  [body(): pl.pallas_call(kernel, out_shape=(jax.ShapeDtypeStruct((2, FD, BINS), F32...]
    unnamed x4 -> x2, local copies, waits for them, and re-layouts: 2.08 us -> 1.23 us
where the time goes in v4:
time: 55.5 us; the launch traced here: 55.3 us
  Pallas kernels  53.5 us (96%)
  local copies, waits for them, and re-layouts  1.23 us (2%)
  between operations  0.64 us (1%)
    pallas_call x1, Pallas kernels, body(): pl.pallas_call(kernel, out_shape=(jax.ShapeDtypeStruct((2, FD, BINS), F32...  53.5 us
    unnamed x2, local copies, waits for them, and re-layouts  1.23 us

profile of v4, /device:TPU:1, one launch (start us, length us, event | category | flops | bytes accessed | tf_op | source)
XLA Modules:
  0.0 55.3 jit_solution(1898447512849690342)
XLA Ops:
  0.6 53.5 %shard_map.86 = (f32[2,64,64]{2,1,0:T(8,128)S(1)}, f32[16,64]{1,0:T(8,128)S(1)}) custom-call(s32[8]{0:T(128)} %sf_hbm.1, s32[8]{0:T(128)} %sb_hbm.1, f32[32,192]{1,0:T(8,128)} %bitcast.6, s32[1,192]{1,0:T(1,128)} %bitcast.7, s32[64,3072]{1,0:T(8,128)} %bins_hbm.1, s32[24,128]{1,0:T(8,128)} %bitcast.4, s32[1,3072]{1,0:T(1,128)} %bitcast.5, f32[16,32]{1,0:T(8,128)} %leaf_hbm.1), custom_call_target="tpu_custom_call" | custom-call | tf_op jit(solution)/shard_map/pallas_call | solution.py:480
  54.1 0.6 %copy.11 = f32[2,64,64]{2,1,0:T(8,128)} copy(f32[2,64,64]{2,1,0:T(8,128)S(1)} %get-tuple-element.4) | data formatting | bytes 65536
  54.7 0.6 %copy.12 = f32[16,64]{1,0:T(8,128)} copy(f32[16,64]{1,0:T(8,128)S(1)} %get-tuple-element.5) | data formatting | bytes 8192

commit v5 on v4

--- a/solution.py
+++ b/solution.py
@@ -22,7 +22,7 @@
 FL = FD // NR
 FAR_FIRST = (10, 6, 14, 9, 11, 8, 2, 5, 7, 13, 15, 4, 12, 1, 3)
 ROW_ORDER = ((0, 1), (1, 0), (1, 1), (3, 0), (3, 1), (2, 0), (2, 1))
-FAR_ROWS = (5, 6, 1, 2, 3, 4, 0)
+CHIP = 4
 BF = jnp.bfloat16
 F32 = jnp.float32
 
@@ -45,7 +45,7 @@
     sf_hbm, sb_hbm, margin_hbm, label_hbm, bins_hbm, par_hbm, parrow_hbm, leaf_hbm,
     gain_ref, total_ref,
     sf_ref, sb_ref, margin_ref, label_ref, bins_ref, par_ref, parrow_ref, leaf_ref,
-    bit_f32, bit_send, bit_recv, bin_send, bin_recv, bin_all, node_all,
+    bit_f32, bit_send, bit_recv, bin_send, bin_recv, bin_all, node_all, node_rel,
     spec, grads, acc, chunk_tot, group_tot, gain_send, gain_recv,
     in_sem, bit_ss, bit_rs, bin_ss, bin_rs, node_ss, node_rs, x_ss, x_rs,
     z_ss, z_rs, y_ss, y_rs, far_ss, far_rs, sib_ss, sib_rs, out_ss, out_rs,
@@ -196,6 +196,11 @@
         arrived(block(core, order(i), 2), far_rs.at[i])
         sib_copy(2, i).start()
 
+    def renumber(r):
+        nodes = node_all[r] - (CHIP * (y + 1)).astype(F32)
+        nodes = jnp.where(nodes < 0, nodes + NODES, nodes)
+        node_rel[r] = jnp.where(nodes < 0, nodes + NODES, nodes)
+
     def row_arrival(d):
         bin_copy(d).wait_recv()
         dy, other = ROW_ORDER[d]
@@ -204,6 +209,7 @@
         for k in range(KB):
             bin_all[came, k] = part[k * FL : (k + 1) * FL]
         arrived(node_all.at[came], node_rs.at[d])
+        renumber(came)
 
     pl.semaphore_wait(barrier, NF - 1 + NR - 1)
     for d in FAR_FIRST:
@@ -223,6 +229,7 @@
         bit_copy(d).wait_recv()
         bits = bits + bit_recv[d].astype(F32)
     node_all[row] = (2 * par_ref[...]).astype(F32) + bits[:KB]
+    renumber(row)
     bit_f32[...] = bits
     for d in range(NR - 1):
         node_copy(d).start()
@@ -259,19 +266,19 @@
         high = pltpu.roll(high, 64, 1).astype(BF)
         return even[:64], jnp.concatenate([low, high], axis=0), last[:64]
 
-    def accumulate(blocks):
+    def accumulate(blocks, low, high):
         weighted, masks = [], []
         for half, zz, yy in blocks:
             group = 2 * yy + half
             for q in range(2):
                 first = 3 * (2 * zz + q)
                 for i, piece in enumerate(pair_pieces(half, zz, yy, q)):
-                    nodes = node_all[group, pl.ds(first + i, 1), :].astype(BF)
+                    nodes = node_rel[group, pl.ds(first + i, 1), :].astype(BF)
                     wide = jnp.broadcast_to(nodes, (COLS, LANES))
                     zero = jnp.zeros_like(piece)
                     weighted.append(
                         jnp.concatenate(
-                            [jnp.where(wide == BF(n), piece, zero) for n in range(NODES)],
+                            [jnp.where(wide == BF(n), piece, zero) for n in range(low, high)],
                             axis=0,
                         )
                     )
@@ -281,7 +288,7 @@
                         under = jnp.broadcast_to(here, (BINS, LANES)) <= bin_ids
                         rows.append(jnp.where(under, BF(1), BF(0)))
                     masks.append(jnp.concatenate(rows, axis=0))
-        acc[...] += lax.dot_general(
+        acc[low * COLS : high * COLS] += lax.dot_general(
             jnp.concatenate(weighted, axis=1),
             jnp.concatenate(masks, axis=1),
             contract,
@@ -318,7 +325,7 @@
         def _():
             sib_wait(0, 0)
 
-        accumulate([((core + u) % 2, z, y)])
+        accumulate([((core + u) % 2, z, y)], 0, NODES)
         return carry
 
     lax.fori_loop(0, 2, first, 0)
@@ -338,7 +345,7 @@
             sib_wait(0, 2)
 
         half = (core + u) % 2
-        accumulate([(half, (z + 1) % 4, y), (half, (z + 3) % 4, y)])
+        accumulate([(half, (z + 1) % 4, y), (half, (z + 3) % 4, y)], 0, NODES)
         return carry
 
     lax.fori_loop(0, 2, near, 0)
@@ -357,83 +364,108 @@
     for d in range(NR - 1):
         group_tot_copy(d).start()
 
-    def beyond(s, carry):
-        @pl.when(s == 0)
-        def _():
-            y_arrival(1)
-            sib_wait(3, 0)
-            sib_wait(1, 0)
-
-        @pl.when(s == 1)
-        def _():
-            y_arrival(2)
-            sib_wait(3, 1)
-            sib_wait(1, 1)
-
-        @pl.when(s == 2)
-        def _():
-            y_arrival(3)
-            far_arrival(0)
-            far_arrival(1)
-            sib_wait(3, 2)
-            sib_wait(1, 2)
-
-        @pl.when(s == 3)
-        def _():
-            far_arrival(2)
-            far_arrival(3)
-            sib_wait(3, 3)
-            sib_wait(1, 3)
-
-        @pl.when(s == 4)
-        def _():
-            sib_wait(2, 0)
-            sib_wait(2, 1)
-
-        @pl.when(s == 5)
-        def _():
-            sib_wait(2, 2)
-            sib_wait(2, 3)
-
+    def beyond_blocks(s):
         far = s // 4
         blocks = []
         for j in range(4):
             dy = (1 - far) * (3 - 2 * (j % 2)) + 2 * far
             i = (1 - far) * s + far * (2 * (s - 4) + j % 2)
             blocks.append(((core + j // 2) % 2, (z + order(i)) % 4, (y + dy) % 4))
-        accumulate(blocks)
+        return blocks
+
+    def early(s, carry):
+        @pl.when(s == 0)
+        def _():
+            y_arrival(1)
+            sib_wait(3, 0)
+            sib_wait(1, 0)
+
+        @pl.when(s == 1)
+        def _():
+            y_arrival(2)
+            sib_wait(3, 1)
+            sib_wait(1, 1)
+
+        accumulate(beyond_blocks(s), 0, NODES)
         return carry
 
-    lax.fori_loop(0, 6, beyond, 0)
+    lax.fori_loop(0, 2, early, 0)
 
     sib_wait(0, 3)
-    accumulate([(core, (z + 2) % 4, y), (1 - core, (z + 2) % 4, y)])
-
-    for n in range(NODES):
-        base = n * COLS
-        gl = acc[base : base + CLASSES, :]
-        hl = acc[base + CLASSES : base + COLS, :]
-        whole_g = acc[base : base + CLASSES, BINS - 1 : BINS]
-        whole_h = acc[base + CLASSES : base + COLS, BINS - 1 : BINS]
-        gr = whole_g - gl
-        hr = whole_h - hl
-        score = (
-            gl * gl / (hl + RIDGE)
-            + gr * gr / (hr + RIDGE)
-            - whole_g * whole_g / (whole_h + RIDGE)
-        )
-        gain = jnp.sum(score, axis=0, keepdims=True) * (1.0 / CLASSES)
-        for k in range(4):
-            at = (n % 2) * 4 + k
-            gain_send[n // 2, at : at + 1, :] = gain[:, k * LANES : (k + 1) * LANES]
-
-    def out_copy(d):
-        to = row_at(*ROW_ORDER[d])
-        return send(gain_send.at[to], gain_recv.at[row], out_ss.at[d], out_rs.at[d], to, feat)
-
-    for d in FAR_ROWS:
-        out_copy(d).start()
-    gain_recv[row] = gain_send[row]
+    accumulate([(core, (z + 2) % 4, y), (1 - core, (z + 2) % 4, y)], 0, NODES)
+
+    def late(s, carry):
+        @pl.when(s == 2)
+        def _():
+            y_arrival(3)
+            far_arrival(0)
+            far_arrival(1)
+            sib_wait(3, 2)
+            sib_wait(1, 2)
+
+        @pl.when(s == 3)
+        def _():
+            far_arrival(2)
+            far_arrival(3)
+            sib_wait(3, 3)
+            sib_wait(1, 3)
+
+        @pl.when(s == 4)
+        def _():
+            sib_wait(2, 0)
+            sib_wait(2, 1)
+
+        @pl.when(s == 5)
+        def _():
+            sib_wait(2, 2)
+            sib_wait(2, 3)
+
+        accumulate(beyond_blocks(s), 0, NODES - CHIP)
+        return carry
+
+    lax.fori_loop(2, 6, late, 0)
+
+    def gains(low, high):
+        for n in range(low, high):
+            base = n * COLS
+            gl = acc[base : base + CLASSES, :]
+            hl = acc[base + CLASSES : base + COLS, :]
+            whole_g = acc[base : base + CLASSES, BINS - 1 : BINS]
+            whole_h = acc[base + CLASSES : base + COLS, BINS - 1 : BINS]
+            gr = whole_g - gl
+            hr = whole_h - hl
+            score = (
+                gl * gl / (hl + RIDGE)
+                + gr * gr / (hr + RIDGE)
+                - whole_g * whole_g / (whole_h + RIDGE)
+            )
+            gain = jnp.sum(score, axis=0, keepdims=True) * (1.0 / CLASSES)
+            for k in range(4):
+                at = (n % 2) * 4 + k
+                gain_send[n // 2, at : at + 1, :] = gain[:, k * LANES : (k + 1) * LANES]
+
+    def out_copy(pair):
+        to = 2 * ((y + 1 + pair // 2) % 4) + pair % 2
+        at = out_rs.at[2 * (pair // 2) + core]
+        return send(gain_send.at[pair], gain_recv.at[row], out_ss.at[pair], at, to, feat)
+
+    def out_sib_copy():
+        at = gain_send.at[NR - 1 - core]
+        return send(at, gain_recv.at[row], out_ss.at[NR - 1], out_rs.at[NR - 1], row_at(0, 1), feat)
+
+    gains(0, NODES - CHIP)
+    for pair in (2, 3, 0, 1, 4, 5):
+        out_copy(pair).start()
+
+    def rest(s, carry):
+        accumulate(beyond_blocks(s), NODES - CHIP, NODES)
+        return carry
+
+    lax.fori_loop(2, 6, rest, 0)
+    gains(NODES - CHIP, NODES)
+    out_sib_copy().start()
+    gain_recv[row] = gain_send[NR - 2 + core]
+
     for d in range(NR - 1):
         dy, other = ROW_ORDER[d]
         arrived(group_tot.at[row_at(4 - dy, other)], gt_rs.at[d])
@@ -442,9 +474,11 @@
         totals = totals + group_tot[r]
     total_ref[...] = totals
 
-    for d in range(NR - 1):
-        dy, other = ROW_ORDER[d]
-        arrived(gain_recv.at[row_at(4 - dy, other)], out_rs.at[d])
+    for k in range(3):
+        for other in range(2):
+            came = 2 * ((y + 3 - k) % 4) + other
+            arrived(gain_recv.at[came], out_rs.at[2 * k + other])
+    arrived(gain_recv.at[row_at(0, 1)], out_rs.at[NR - 1])
     for r in range(NR):
         for n in range(2):
             tile = gain_recv[r, 4 * n : 4 * n + 4, :]
@@ -457,8 +491,10 @@
     for d in range(NR - 1):
         bin_copy(d).wait_send()
         node_copy(d).wait_send()
-        out_copy(d).wait_send()
         group_tot_copy(d).wait_send()
+    for pair in range(6):
+        out_copy(pair).wait_send()
+    out_sib_copy().wait_send()
     for d in range(1, 4):
         x_copy(d).wait_send()
         chunk_tot_copy(d).wait_send()
@@ -500,6 +536,7 @@
             pltpu.VMEM((NR, KB * FL, LANES), BF),
             pltpu.VMEM((NR, KB * FL, LANES), BF),
             pltpu.VMEM((NR, KB, FL, LANES), F32),
+            pltpu.VMEM((NR, KB, LANES), F32),
             pltpu.VMEM((NR, KB, LANES), F32),
             pltpu.VMEM((4, 2, 96, LANES), BF),
             pltpu.VMEM((2, 4, 4, 4, 96, LANES), BF),

time: 55.5 us -> 54.1 us (0.975)
  Pallas kernels: 53.5 us -> 52.1 us
    pallas_call x1, Pallas kernels: 53.5 us -> 52.1 us  [body(): pl.pallas_call(kernel, out_shape=(jax.ShapeDtypeStruct((2, FD, BINS), F32...]
where the time goes in v5:
time: 54.1 us; the launch traced here: 54 us
  Pallas kernels  52.1 us (96%)
  local copies, waits for them, and re-layouts  1.23 us (2%)
  between operations  0.64 us (1%)
    pallas_call x1, Pallas kernels, body(): pl.pallas_call(kernel, out_shape=(jax.ShapeDtypeStruct((2, FD, BINS), F32...  52.1 us
    unnamed x2, local copies, waits for them, and re-layouts  1.23 us

profile of v5, /device:TPU:1, one launch (start us, length us, event | category | flops | bytes accessed | tf_op | source)
XLA Modules:
  0.0 54.0 jit_solution(12189843494677207858)
XLA Ops:
  0.6 52.1 %shard_map.86 = (f32[2,64,64]{2,1,0:T(8,128)S(1)}, f32[16,64]{1,0:T(8,128)S(1)}) custom-call(s32[8]{0:T(128)} %sf_hbm.1, s32[8]{0:T(128)} %sb_hbm.1, f32[32,192]{1,0:T(8,128)} %bitcast.6, s32[1,192]{1,0:T(1,128)} %bitcast.7, s32[64,3072]{1,0:T(8,128)} %bins_hbm.1, s32[24,128]{1,0:T(8,128)} %bitcast.4, s32[1,3072]{1,0:T(1,128)} %bitcast.5, f32[16,32]{1,0:T(8,128)} %leaf_hbm.1), custom_call_target="tpu_custom_call" | custom-call | tf_op jit(solution)/shard_map/pallas_call | solution.py:516
  52.8 0.6 %copy.11 = f32[2,64,64]{2,1,0:T(8,128)} copy(f32[2,64,64]{2,1,0:T(8,128)S(1)} %get-tuple-element.4) | data formatting | bytes 65536
  53.4 0.6 %copy.12 = f32[16,64]{1,0:T(8,128)} copy(f32[16,64]{1,0:T(8,128)S(1)} %get-tuple-element.5) | data formatting | bytes 8192

commit v6 on v5

--- a/solution.py
+++ b/solution.py
@@ -341,6 +341,7 @@
 
         @pl.when(u == 1)
         def _():
+            y_arrival(0)
             sib_wait(0, 1)
             sib_wait(0, 2)
 
@@ -353,7 +354,6 @@
     for way in range(2):
         arrived(block(core, 2, 0).at[pl.ds(2 * way, 2)], z_rs.at[2 + way])
     pass_on(3)
-    y_arrival(0)
 
     for d in range(1, NR - 1):
         row_arrival(d)
@@ -364,66 +364,62 @@
     for d in range(NR - 1):
         group_tot_copy(d).start()
 
-    def beyond_blocks(s):
-        far = s // 4
+    def other_y(half, k):
+        far = k // 4
         blocks = []
-        for j in range(4):
-            dy = (1 - far) * (3 - 2 * (j % 2)) + 2 * far
-            i = (1 - far) * s + far * (2 * (s - 4) + j % 2)
-            blocks.append(((core + j // 2) % 2, (z + order(i)) % 4, (y + dy) % 4))
+        for j in range(2):
+            dy = (1 - far) * (3 - 2 * j) + 2 * far
+            i = (1 - far) * k + far * (2 * (k - 4) + j)
+            blocks.append((half, (z + order(i)) % 4, (y + dy) % 4))
         return blocks
 
-    def early(s, carry):
-        @pl.when(s == 0)
-        def _():
-            y_arrival(1)
-            sib_wait(3, 0)
-            sib_wait(1, 0)
-
-        @pl.when(s == 1)
+    def step_blocks(k):
+        return other_y(core, k) + other_y(1 - core, k - 1)
+
+    sib_wait(3, 0)
+    sib_wait(1, 0)
+    accumulate(other_y(core, 0) + other_y(1 - core, 0), 0, NODES)
+
+    y_arrival(1)
+    sib_wait(0, 3)
+    last_z = [(core, (z + 2) % 4, y), (1 - core, (z + 2) % 4, y)]
+    accumulate(other_y(core, 1) + last_z, 0, NODES)
+
+    def late(k, carry):
+        @pl.when(k == 2)
         def _():
             y_arrival(2)
             sib_wait(3, 1)
             sib_wait(1, 1)
 
-        accumulate(beyond_blocks(s), 0, NODES)
-        return carry
-
-    lax.fori_loop(0, 2, early, 0)
-
-    sib_wait(0, 3)
-    accumulate([(core, (z + 2) % 4, y), (1 - core, (z + 2) % 4, y)], 0, NODES)
-
-    def late(s, carry):
-        @pl.when(s == 2)
+        @pl.when(k == 3)
         def _():
             y_arrival(3)
+            sib_wait(3, 2)
+            sib_wait(1, 2)
+
+        @pl.when(k == 4)
+        def _():
             far_arrival(0)
             far_arrival(1)
-            sib_wait(3, 2)
-            sib_wait(1, 2)
-
-        @pl.when(s == 3)
+            sib_wait(3, 3)
+            sib_wait(1, 3)
+
+        @pl.when(k == 5)
         def _():
             far_arrival(2)
             far_arrival(3)
-            sib_wait(3, 3)
-            sib_wait(1, 3)
-
-        @pl.when(s == 4)
-        def _():
             sib_wait(2, 0)
             sib_wait(2, 1)
 
-        @pl.when(s == 5)
-        def _():
-            sib_wait(2, 2)
-            sib_wait(2, 3)
-
-        accumulate(beyond_blocks(s), 0, NODES - CHIP)
+        accumulate(step_blocks(k), 0, NODES - CHIP)
         return carry
 
     lax.fori_loop(2, 6, late, 0)
+
+    sib_wait(2, 2)
+    sib_wait(2, 3)
+    accumulate(other_y(1 - core, 5), 0, NODES)
 
     def gains(low, high):
         for n in range(low, high):
@@ -457,8 +453,8 @@
     for pair in (2, 3, 0, 1, 4, 5):
         out_copy(pair).start()
 
-    def rest(s, carry):
-        accumulate(beyond_blocks(s), NODES - CHIP, NODES)
+    def rest(k, carry):
+        accumulate(step_blocks(k), NODES - CHIP, NODES)
         return carry
 
     lax.fori_loop(2, 6, rest, 0)

time: 54.1 us -> 52.2 us (0.965)
  Pallas kernels: 52.1 us -> 50.2 us
    pallas_call x1, Pallas kernels: 52.1 us -> 50.2 us  [body(): pl.pallas_call(kernel, out_shape=(jax.ShapeDtypeStruct((2, FD, BINS), F32...]
where the time goes in v6:
time: 52.2 us; the launch traced here: 52.1 us
  Pallas kernels  50.2 us (96%)
  local copies, waits for them, and re-layouts  1.23 us (2%)
  between operations  0.64 us (1%)
    pallas_call x1, Pallas kernels, body(): pl.pallas_call(kernel, out_shape=(jax.ShapeDtypeStruct((2, FD, BINS), F32...  50.2 us
    unnamed x2, local copies, waits for them, and re-layouts  1.23 us

profile of v6, /device:TPU:1, one launch (start us, length us, event | category | flops | bytes accessed | tf_op | source)
XLA Modules:
  0.0 52.1 jit_solution(1343598527326594558)
XLA Ops:
  0.6 50.2 %shard_map.86 = (f32[2,64,64]{2,1,0:T(8,128)S(1)}, f32[16,64]{1,0:T(8,128)S(1)}) custom-call(s32[8]{0:T(128)} %sf_hbm.1, s32[8]{0:T(128)} %sb_hbm.1, f32[32,192]{1,0:T(8,128)} %bitcast.6, s32[1,192]{1,0:T(1,128)} %bitcast.7, s32[64,3072]{1,0:T(8,128)} %bins_hbm.1, s32[24,128]{1,0:T(8,128)} %bitcast.4, s32[1,3072]{1,0:T(1,128)} %bitcast.5, f32[16,32]{1,0:T(8,128)} %leaf_hbm.1), custom_call_target="tpu_custom_call" | custom-call | tf_op jit(solution)/shard_map/pallas_call | solution.py:512
  50.9 0.6 %copy.11 = f32[2,64,64]{2,1,0:T(8,128)} copy(f32[2,64,64]{2,1,0:T(8,128)S(1)} %get-tuple-element.4) | data formatting | bytes 65536
  51.5 0.6 %copy.12 = f32[16,64]{1,0:T(8,128)} copy(f32[16,64]{1,0:T(8,128)S(1)} %get-tuple-element.5) | data formatting | bytes 8192

commit v7 on v6

--- a/solution.py
+++ b/solution.py
@@ -49,7 +49,7 @@
     spec, grads, acc, chunk_tot, group_tot, gain_send, gain_recv,
     in_sem, bit_ss, bit_rs, bin_ss, bin_rs, node_ss, node_rs, x_ss, x_rs,
     z_ss, z_rs, y_ss, y_rs, far_ss, far_rs, sib_ss, sib_rs, out_ss, out_rs,
-    ct_ss, ct_rs, gt_ss, gt_rs,
+    ct_ss, ct_rs, gt_ss, gt_rs, y_ready,
 ):
     row = lax.axis_index("rows")
     feat = lax.axis_index("feat")
@@ -66,8 +66,26 @@
     barrier = pltpu.get_barrier_semaphore()
     for d in FAR_FIRST:
         pl.semaphore_signal(barrier, inc=1, device_id=(row, (feat + d) % NF), device_id_type=MESH)
-    for d in range(1, NR):
-        pl.semaphore_signal(barrier, inc=1, device_id=((row + d) % NR, feat), device_id_type=MESH)
+    pl.semaphore_signal(
+        barrier, inc=1, device_id=(row + 1 - 2 * core, feat), device_id_type=MESH
+    )
+
+    def rank(yy):
+        return yy + yy // 2 - 2 * (yy // 3)
+
+    def greet_y(sem, up):
+        for dy in range(1, 4):
+            there = (y + dy) % 4
+            ahead = rank(there) > rank(y) if up else rank(there) < rank(y)
+            for c in range(2):
+
+                @pl.when(ahead)
+                def _():
+                    pl.semaphore_signal(
+                        sem, inc=1, device_id=(2 * there + c, feat), device_id_type=MESH
+                    )
+
+    greet_y(barrier, True)
 
     inputs = [
         pltpu.make_async_copy(src, dst, in_sem.at[k])
@@ -211,11 +229,17 @@
         arrived(node_all.at[came], node_rs.at[d])
         renumber(came)
 
-    pl.semaphore_wait(barrier, NF - 1 + NR - 1)
+    pl.semaphore_wait(barrier, NF + 2 * rank(y))
+    greet_y(y_ready, False)
     for d in FAR_FIRST:
         bit_copy(d).start()
     for d in (1, 3, 2):
         x_copy(d).start()
+
+    @pl.when(rank(y) < 3)
+    def _():
+        pl.semaphore_wait(y_ready, 2 * (3 - rank(y)))
+
     for d, (dy, other) in enumerate(ROW_ORDER):
         bin_send[d] = jnp.concatenate(load_bins(row_at(dy, other)), axis=0).astype(BF)
         bin_copy(d).start()
@@ -547,6 +571,7 @@
             dma((2, 4)), dma((2, 4)), dma((4,)), dma((4,)), dma((4, 4)), dma((4, 4)),
             dma((NR,)), dma((NR,)),
             dma((4,)), dma((4,)), dma((NR,)), dma((NR,)),
+            pltpu.SemaphoreType.REGULAR,
         ],
         compiler_params=pltpu.CompilerParams(
             collective_id=0, has_side_effects=True, vmem_limit_bytes=48 << 20

time: 52.2 us -> 51.8 us (level)
  no operation moved by 1% of the time
where the time goes in v7:
time: 51.8 us; the launch traced here: 51.7 us
  Pallas kernels  49.8 us (96%)
  local copies, waits for them, and re-layouts  1.23 us (2%)
  between operations  0.64 us (1%)
    pallas_call x1, Pallas kernels, body(): pl.pallas_call(kernel, out_shape=(jax.ShapeDtypeStruct((2, FD, BINS), F32...  49.8 us
    unnamed x2, local copies, waits for them, and re-layouts  1.23 us

profile of v7, /device:TPU:1, one launch (start us, length us, event | category | flops | bytes accessed | tf_op | source)
XLA Modules:
  0.0 51.7 jit_solution(11728036987948662883)
XLA Ops:
  0.6 49.8 %shard_map.86 = (f32[2,64,64]{2,1,0:T(8,128)S(1)}, f32[16,64]{1,0:T(8,128)S(1)}) custom-call(s32[8]{0:T(128)} %sf_hbm.1, s32[8]{0:T(128)} %sb_hbm.1, f32[32,192]{1,0:T(8,128)} %bitcast.6, s32[1,192]{1,0:T(1,128)} %bitcast.7, s32[64,3072]{1,0:T(8,128)} %bins_hbm.1, s32[24,128]{1,0:T(8,128)} %bitcast.4, s32[1,3072]{1,0:T(1,128)} %bitcast.5, f32[16,32]{1,0:T(8,128)} %leaf_hbm.1), custom_call_target="tpu_custom_call" | custom-call | tf_op jit(solution)/shard_map/pallas_call | solution.py:536
  50.5 0.6 %copy.11 = f32[2,64,64]{2,1,0:T(8,128)} copy(f32[2,64,64]{2,1,0:T(8,128)S(1)} %get-tuple-element.4) | data formatting | bytes 65536
  51.1 0.6 %copy.12 = f32[16,64]{1,0:T(8,128)} copy(f32[16,64]{1,0:T(8,128)S(1)} %get-tuple-element.5) | data formatting | bytes 8192
